TPU v7x, 256 devices: a whole 4x4x8 slice. The times are simulated.
256 devices in a mesh: qa: 8 (over y, z_hi), qb: 32 (over x, z_lo, core).
Axes of the slice: x: 4, y: 4, z: 8 (z_hi: 2, z_lo: 4; z = z_hi * 4 + z_lo), core: 2. Of those that a mesh axis runs over, the one named last changes fastest.
Arguments:
- state: float32 [2, 8, 32, 65536], P(None, 'qa', 'qb'), may hold values from -6 to 6
- adjoint: float32 [2, 8, 32, 65536], P(None, 'qa', 'qb'), may hold values from -6 to 6
- gates: float32 [8, 2, 128, 128], replicated, may hold values from -1 to 1, as said below
Outputs:
- state_out: float32 [2, 8, 32, 65536], P(None, 'qa', 'qb')
- adjoint_out: float32 [2, 8, 32, 65536], P(None, 'qa', 'qb')
- gate_grads: float32 [8, 2, 128, 128], replicated
Inputs may be any that keep to these rules, and one draw needn't show every extreme that they name: gates[k, 0] + i gates[k, 1] is a unitary 128 x 128 matrix for every k.
All inputs are finite; a program needn't handle non-finite values.
Results may differ from a plain program's by a relative error of at most 0.0001.
Values sent between devices are 32-bit elements; how exact they have to be, the bound alone decides.
A program may use at most 64 MiB of HBM per device.

v0:
```python
import jax
import jax.numpy as jnp
from jax import lax
from jax.sharding import PartitionSpec as P

precise = lax.Precision.HIGHEST


def sent_together(arrays, axis, split_dim, concat_dim, along):
    both = jnp.concatenate(arrays, axis=along)
    result, at, finished = (
        lax.all_to_all(both, axis, split_axis=split_dim, concat_axis=concat_dim, tiled=True),
        0,
        [],
    )
    for a in arrays:
        finished.append(lax.slice_in_dim(result, at, at + a.shape[along], axis=along))
        at += a.shape[along]
    return tuple(finished)


def contract(left, right, left_dim, right_dim):
    return lax.dot_general(
        left,
        right,
        (((left_dim,), (right_dim,)), ((), ())),
        precision=precise,
        preferred_element_type=jnp.float32,
    )


def undo_high(field, gate):
    new_real = contract(gate[0], field[0], 0, 0) + contract(gate[1], field[1], 0, 0)
    new_imag = contract(gate[0], field[1], 0, 0) - contract(gate[1], field[0], 0, 0)
    return jnp.stack([new_real, new_imag])


def undo_low(field, gate):
    new_real = contract(field[0], gate[0], 1, 0) + contract(field[1], gate[1], 1, 0)
    new_imag = contract(field[1], gate[0], 1, 0) - contract(field[0], gate[1], 1, 0)
    return jnp.stack([new_real, new_imag])


def pair_high(adjoint_field, new_field):
    grad_real = contract(adjoint_field[0], new_field[0], 1, 1) + contract(
        adjoint_field[1], new_field[1], 1, 1
    )
    grad_imag = contract(adjoint_field[1], new_field[0], 1, 1) - contract(
        adjoint_field[0], new_field[1], 1, 1
    )
    return jnp.stack([grad_real, grad_imag])


def pair_low(adjoint_field, new_field):
    grad_real = contract(adjoint_field[0], new_field[0], 0, 0) + contract(
        adjoint_field[1], new_field[1], 0, 0
    )
    grad_imag = contract(adjoint_field[1], new_field[0], 0, 0) - contract(
        adjoint_field[0], new_field[1], 0, 0
    )
    return jnp.stack([grad_real, grad_imag])


def shards(state, adjoint, gates):
    gate_size = gates.shape[-1]
    local_count = state.shape[-1]
    scaling = float(lax.axis_size("qa") * lax.axis_size("qb") * local_count // gate_size) ** (-0.5)
    state_now = state.reshape(2, local_count)
    adjoint_now = adjoint.reshape(2, local_count)
    collected = []
    for section in range(gates.shape[0] // 2):
        high_gate = gates[2 * section]
        low_gate = gates[2 * section + 1]
        upright = (2, gate_size, local_count // gate_size)
        state_high = state_now.reshape(upright)
        adjoint_high = adjoint_now.reshape(upright)
        state_new = undo_high(state_high, high_gate)
        collected.append(scaling * pair_high(adjoint_high, state_new))
        adjoint_new = undo_high(adjoint_high, high_gate)
        flat = (2, local_count // gate_size, gate_size)
        state_low = state_new.reshape(flat)
        adjoint_low = adjoint_new.reshape(flat)
        groups = lax.axis_size("qa") if section % 2 == 0 else lax.axis_size("qb")
        state_done = undo_low(state_low, low_gate)
        collected.append(scaling * pair_low(adjoint_low, state_done))
        adjoint_done = undo_low(adjoint_low, low_gate)
        split = (2, groups, local_count // groups)
        outgoing = (state_done.reshape(split), adjoint_done.reshape(split))
        if section % 2 == 0:
            arrived = (
                lax.all_to_all(outgoing[0], "qa", split_axis=1, concat_axis=1, tiled=True),
                lax.all_to_all(outgoing[1], "qa", split_axis=1, concat_axis=1, tiled=True),
            )
        else:
            arrived = sent_together((outgoing[0], outgoing[1]), "qb", 1, 1, 0)
        state_now = arrived[0].reshape(2, local_count)
        adjoint_now = arrived[1].reshape(2, local_count)
    gradients = lax.psum(jnp.stack(collected), ("qa", "qb"))
    return (state_now.reshape(state.shape), adjoint_now.reshape(adjoint.shape), gradients)


def solution(mesh):
    in_specs = (P(None, "qa", "qb", None), P(None, "qa", "qb", None), P())
    out_specs = (P(None, "qa", "qb", None), P(None, "qa", "qb", None), P())
    return jax.shard_map(shards, mesh=mesh, in_specs=in_specs, out_specs=out_specs, check_vma=False)
```

profile of v0, /device:TPU:1, one launch (start us, length us, event | category | flops | bytes accessed | tf_op | source)
XLA Modules:
  0.0 466.4 jit_solution(3759469993597198307)
XLA Ops:
  7.2 3.9 slice_reduce_fusion.13
  11.2 1.1 copy-done
  15.6 1.3 pad_maximum_fusion.3
  16.9 12.0 %all-to-all-start.1 = ((f32[2,8,8192]{2,0,1:T(2,128)}), f32[2,8,8192]{2,0,1:T(2,128)S(1)}, u32[]{:S(2)}, u32[]{:S(2)}) async-start(f32[2,8,8192]{2,0,1:T(2,128)} %pad_maximum_fusion.3), calls=%async_computation.1 | async-start | bytes 1048576 | tf_op jit(solution)/shard_map/all_to_all | solution.py:92
  29.3 1.1 fusion.122
  32.3 1.4 convolution_subtract_fusion.15
  38.7 1.2 fusion.19
  39.9 1.3 pad_maximum_fusion.2
  41.1 2.0 all-to-all-done.1
  43.1 7.5 %all-to-all-start = ((f32[2,8,8192]{2,0,1:T(2,128)}), f32[2,8,8192]{2,0,1:T(2,128)S(1)}, u32[]{:S(2)}, u32[]{:S(2)}) async-start(f32[2,8,8192]{2,0,1:T(2,128)} %pad_maximum_fusion.2), calls=%async_computation | async-start | bytes 1048576 | tf_op jit(solution)/shard_map/all_to_all | solution.py:91
  50.7 1.3 slice_reduce_fusion.9
  57.7 5.2 %all-to-all-done = f32[2,8,8192]{2,0,1:T(2,128)S(1)} async-done(((f32[2,8,8192]{2,0,1:T(2,128)}), f32[2,8,8192]{2,0,1:T(2,128)S(1)}, u32[]{:S(2)}, u32[]{:S(2)}) %all-to-all-start) | async-done | bytes 524320 | tf_op jit(solution)/shard_map/all_to_all | solution.py:91
  62.9 1.6 slice_reduce_fusion.11
  70.7 2.1 pad_maximum_fusion
  72.8 14.2 %all-to-all-start.2 = ((f32[4,32,2048]{2,0,1:T(4,128)}), f32[4,32,2048]{2,0,1:T(4,128)S(1)}, u32[]{:S(2)}, u32[]{:S(2)}) async-start(f32[4,32,2048]{2,0,1:T(4,128)} %pad_maximum_fusion), calls=%async_computation.2 | async-start | bytes 2097152 | tf_op jit(solution)/shard_map/all_to_all | solution.py:12
  87.0 1.5 fusion.22
  97.6 17.3 %all-to-all-done.2 = f32[4,32,2048]{2,0,1:T(4,128)S(1)} async-done(((f32[4,32,2048]{2,0,1:T(4,128)}), f32[4,32,2048]{2,0,1:T(4,128)S(1)}, u32[]{:S(2)}, u32[]{:S(2)}) %all-to-all-start.2) | async-done | bytes 1048608 | tf_op jit(solution)/shard_map/all_to_all | solution.py:12
  114.9 2.8 slice_reduce_fusion.7
  133.0 1.3 pad_maximum_fusion.5
  134.3 3.5 all-to-all-start.4
  139.1 1.3 pad_maximum_fusion.4
  140.4 13.9 %all-to-all-done.4 = f32[2,8,8192]{2,0,1:T(2,128)S(1)} async-done(((f32[2,8,8192]{2,0,1:T(2,128)}), f32[2,8,8192]{2,0,1:T(2,128)S(1)}, u32[]{:S(2)}, u32[]{:S(2)}) %all-to-all-start.4) | async-done | bytes 524320 | tf_op jit(solution)/shard_map/all_to_all | solution.py:92
  154.2 5.2 %all-to-all-start.3 = ((f32[2,8,8192]{2,0,1:T(2,128)}), f32[2,8,8192]{2,0,1:T(2,128)S(1)}, u32[]{:S(2)}, u32[]{:S(2)}) async-start(f32[2,8,8192]{2,0,1:T(2,128)} %pad_maximum_fusion.4), calls=%async_computation.3 | async-start | bytes 1048576 | tf_op jit(solution)/shard_map/all_to_all | solution.py:91
  159.4 1.3 slice_reduce_fusion.1
  166.5 7.5 %all-to-all-done.3 = f32[2,8,8192]{2,0,1:T(2,128)S(1)} async-done(((f32[2,8,8192]{2,0,1:T(2,128)}), f32[2,8,8192]{2,0,1:T(2,128)S(1)}, u32[]{:S(2)}, u32[]{:S(2)}) %all-to-all-start.3) | async-done | bytes 524320 | tf_op jit(solution)/shard_map/all_to_all | solution.py:91
  173.9 1.3 slice_reduce_fusion.5
  181.5 2.1 pad_maximum_fusion.1
  183.7 9.6 %all-to-all-start.5 = ((f32[4,32,2048]{2,0,1:T(4,128)}), f32[4,32,2048]{2,0,1:T(4,128)S(1)}, u32[]{:S(2)}, u32[]{:S(2)}) async-start(f32[4,32,2048]{2,0,1:T(4,128)} %pad_maximum_fusion.1), calls=%async_computation.5 | async-start | bytes 2097152 | tf_op jit(solution)/shard_map/all_to_all | solution.py:12
  199.4 254.2 %all-reduce.2.cloned.1.call-done = f32[8,2,128,128]{2,3,1,0:T(8,128)} async-done(((f32[8,2,128,128]{2,3,1,0:T(8,128)}), f32[8,2,128,128]{2,3,1,0:T(8,128)}) %all-reduce.2.cloned.1.call-update) | async-done | bytes 1048592 | tf_op jit(solution)/shard_map/psum | solution.py:98
  453.6 2.5 copy.191
  456.7 1.3 copy.190
  458.1 1.3 copy.189
  (185 shorter events, 65.9 us)
Async XLA Ops:
  11.1 1.2 copy-start
  16.9 26.3 %all-to-all-start.1 = ((f32[2,8,8192]{2,0,1:T(2,128)}), f32[2,8,8192]{2,0,1:T(2,128)S(1)}, u32[]{:S(2)}, u32[]{:S(2)}) async-start(f32[2,8,8192]{2,0,1:T(2,128)} %pad_maximum_fusion.3), calls=%async_computation.1 | async-start | bytes 1048576 | tf_op jit(solution)/shard_map/all_to_all | solution.py:92
  35.4 0.8 copy-start.16
  38.6 1.2 copy-start.5
  43.1 19.8 %all-to-all-start = ((f32[2,8,8192]{2,0,1:T(2,128)}), f32[2,8,8192]{2,0,1:T(2,128)S(1)}, u32[]{:S(2)}, u32[]{:S(2)}) async-start(f32[2,8,8192]{2,0,1:T(2,128)} %pad_maximum_fusion.2), calls=%async_computation | async-start | bytes 1048576 | tf_op jit(solution)/shard_map/all_to_all | solution.py:91
  67.4 0.7 copy-start.1
  68.0 0.7 copy-start.3
  69.6 0.7 copy-start.7
  69.6 1.1 copy-start.12
  69.6 1.1 copy-start.14
  70.0 0.7 copy-start.9
  72.8 14.2 %copy-start.17 = (f32[1,1,128,128]{2,3,1,0:T(8,128)S(1)}, f32[1,1,128,128]{2,3,1,0:T(8,128)}, u32[]{:S(2)}) copy-start(f32[1,1,128,128]{2,3,1,0:T(8,128)} %fusion.20) | copy-start | bytes 196612
  72.8 42.0 %all-to-all-start.2 = ((f32[4,32,2048]{2,0,1:T(4,128)}), f32[4,32,2048]{2,0,1:T(4,128)S(1)}, u32[]{:S(2)}, u32[]{:S(2)}) async-start(f32[4,32,2048]{2,0,1:T(4,128)} %pad_maximum_fusion), calls=%async_computation.2 | async-start | bytes 2097152 | tf_op jit(solution)/shard_map/all_to_all | solution.py:12
  87.0 1.6 copy-start.6
  88.6 0.8 copy-start.18
  89.4 1.0 copy-start.4
  90.4 0.9 copy-start.2
  93.2 1.0 copy-start.10
  94.2 0.9 copy-start.8
  134.3 19.9 %all-to-all-start.4 = ((f32[2,8,8192]{2,0,1:T(2,128)}), f32[2,8,8192]{2,0,1:T(2,128)S(1)}, u32[]{:S(2)}, u32[]{:S(2)}) async-start(f32[2,8,8192]{2,0,1:T(2,128)} %pad_maximum_fusion.5), calls=%async_computation.4 | async-start | bytes 1048576 | tf_op jit(solution)/shard_map/all_to_all | solution.py:92
  154.2 19.7 %all-to-all-start.3 = ((f32[2,8,8192]{2,0,1:T(2,128)}), f32[2,8,8192]{2,0,1:T(2,128)S(1)}, u32[]{:S(2)}, u32[]{:S(2)}) async-start(f32[2,8,8192]{2,0,1:T(2,128)} %pad_maximum_fusion.4), calls=%async_computation.3 | async-start | bytes 1048576 | tf_op jit(solution)/shard_map/all_to_all | solution.py:91
  179.2 1.0 copy-start.11
  180.5 1.0 copy-start.13
  180.5 1.0 copy-start.15
  183.7 272.5 %all-to-all-start.5 = ((f32[4,32,2048]{2,0,1:T(4,128)}), f32[4,32,2048]{2,0,1:T(4,128)S(1)}, u32[]{:S(2)}, u32[]{:S(2)}) async-start(f32[4,32,2048]{2,0,1:T(4,128)} %pad_maximum_fusion.1), calls=%async_computation.5 | async-start | bytes 2097152 | tf_op jit(solution)/shard_map/all_to_all | solution.py:12
  193.2 260.4 %all-reduce.2.cloned.1.call-start = ((), (), s32[]{:S(2)}) async-start(), calls=%async_computation.6 | async-start | bytes 2097152 | tf_op jit(solution)/shard_map/psum | solution.py:98
Sparse Core Ops, SparseCore 0:
  199.5 254.0 all-reduce.1
where the time goes:
time: 473 us; the launch traced here: 466 us
  waiting for transfers between devices  300 us (63%)
  matrix products  55 us (12%)
  starting transfers between devices  52 us (11%)
  local copies, waits for them, and re-layouts  28.5 us (6%)
  other arithmetic  15.5 us (3%)
  between operations  15.4 us (3%)
    psum x1, waiting for transfers between devices, shards(): gradients = lax.psum(jnp.stack(collected), ('qa', 'qb'))  254 us
    dot_general x96, matrix products, contract(): lax.dot_general(left, right, (((left_dim,), (right_dim,)), ((), ())), pre...  55 us
    all_to_all x2, starting transfers between devices, sent_together(): lax.all_to_all(both, axis, split_axis=split_dim, concat_axis=concat_dim,...  23.7 us
    all_to_all x2, waiting for transfers between devices, sent_together(): lax.all_to_all(both, axis, split_axis=split_dim, concat_axis=concat_dim,...  17.3 us
    all_to_all x2, waiting for transfers between devices, shards(): lax.all_to_all(outgoing[1], 'qa', split_axis=1, concat_axis=1, tiled=True)  15.9 us
    all_to_all x2, starting transfers between devices, shards(): lax.all_to_all(outgoing[1], 'qa', split_axis=1, concat_axis=1, tiled=True)  15.4 us
    all_to_all x2, starting transfers between devices, shards(): lax.all_to_all(outgoing[0], 'qa', split_axis=1, concat_axis=1, tiled=True)  12.7 us
    all_to_all x2, waiting for transfers between devices, shards(): lax.all_to_all(outgoing[0], 'qa', split_axis=1, concat_axis=1, tiled=True)  12.7 us
  transfers between devices with their start and end apart: 7, of which 6 were waited for; matrix products, arithmetic and copies ran while one was open for 10% of the time, Pallas kernels for 0%

commit v1 on v0

v1 whole, which is shorter than its diff:
```python
import functools

import jax
import jax.numpy as jnp
from jax import lax
from jax.experimental import pallas as pl
from jax.experimental.pallas import tpu as pltpu
from jax.sharding import PartitionSpec as P

F32 = jnp.float32
BF16 = jnp.bfloat16
MESH = pl.DeviceIdType.MESH
N_QA, N_QB, N_DEV = 8, 32, 256
ROWS = N_DEV * 8
GROWS = 5 * 256


def split(x):
    hi = x.astype(BF16)
    return hi, (x - hi.astype(F32)).astype(BF16)


def dot3(a, b, ca, cb):
    ah, al = split(a)
    bh, bl = split(b)
    left = jnp.concatenate([ah, al, ah], axis=ca)
    right = jnp.concatenate([bh, bh, bl], axis=cb)
    return lax.dot_general(left, right, (((ca,), (cb,)), ((), ())), preferred_element_type=F32)


def conj_embed(re, im):
    return jnp.concatenate(
        [jnp.concatenate([re, -im], axis=1), jnp.concatenate([im, re], axis=1)], axis=0
    )


def swap_bits(vs, shift):
    vs = list(vs)
    lane = lax.broadcasted_iota(jnp.int32, vs[0].shape, 1)
    bit = 0
    while (1 << bit) < len(vs):
        stride = 1 << (shift + bit)
        upper = (lane & stride) != 0
        for i in range(len(vs)):
            if i & (1 << bit):
                continue
            k = i | (1 << bit)
            lo, hi = vs[i], vs[k]
            vs[i] = jnp.where(upper, pltpu.roll(hi, stride, 1), lo)
            vs[k] = jnp.where(upper, hi, pltpu.roll(lo, 128 - stride, 1))
        bit += 1
    return vs


def swap_outer(ref):
    def body(b, _):
        at = [pl.ds(pl.multiple_of((a * 32 + b) * 8, 8), 8) for a in range(8)]
        for s, v in zip(at, swap_bits([ref[s, :] for s in at], 4)):
            ref[s, :] = v
        return 0

    lax.fori_loop(0, 32, body, 0, unroll=2)


def swap_inner(ref):
    def body(a, _):
        at = [pl.ds(pl.multiple_of((a * 32 + b) * 8, 8), 8) for b in range(32)]
        for s, v in zip(at, swap_bits([ref[s, :] for s in at], 2)):
            ref[s, :] = v
        return 0

    lax.fori_loop(0, 8, body, 0)


def quadrants(q):
    return q[:128, :128] + q[128:, 128:], q[128:, :128] - q[:128, 128:]


def low_kernel(state_ref, adjoint_ref, gates_ref, y_ref, rho_ref):
    fields = []
    for ref in (state_ref, adjoint_ref):
        fields.append(jnp.concatenate([ref[0], ref[1]], axis=1))
    rho_re, rho_im = quadrants(dot3(fields[1], fields[0], 0, 0))
    rho_ref[0:128, :] = rho_re
    rho_ref[128:256, :] = rho_im
    top = jnp.concatenate([gates_ref[1, 0], -gates_ref[1, 1]], axis=1)
    for k in (3, 5, 7):
        top = dot3(top, conj_embed(gates_ref[k, 0], gates_ref[k, 1]), 1, 0)
    joined = conj_embed(top[:, :128], -top[:, 128:])
    for m in range(4):
        rows = []
        for ref in (state_ref, adjoint_ref):
            rows.append(
                jnp.concatenate([ref[r, pl.ds(m, 128, stride=4), :] for r in range(2)], axis=1)
            )
        out = dot3(joined, jnp.concatenate(rows, axis=0), 0, 1)
        for r in range(2):
            for f in range(2):
                j = r * 4 + f * 2 + m // 2
                y_ref[pl.ds((m % 2) * 1024 + j, 128, stride=8), :] = out[
                    r * 128 : (r + 1) * 128, f * 128 : (f + 1) * 128
                ]


def high_kernel(z_ref, gates_ref, w_ref, grad_ref):
    w_ref[...] = z_ref[...]

    def gate(index, slot):
        embedded = conj_embed(gates_ref[index, 0], gates_ref[index, 1])
        old = []
        for f in range(2):
            old.append(
                jnp.concatenate(
                    [
                        jnp.concatenate(
                            [w_ref[pl.ds(r * 4 + f * 2 + m, 256, stride=8), :] for r in range(2)],
                            axis=1,
                        )
                        for m in range(2)
                    ],
                    axis=0,
                )
            )
        new = [dot3(x, embedded, 1, 0) for x in old]
        grad_re, grad_im = quadrants(dot3(old[1], new[0], 0, 0))
        grad_ref[pl.ds(slot * 256, 128), :] = grad_re
        grad_ref[pl.ds(slot * 256 + 128, 128), :] = grad_im
        for f in range(2):
            for m in range(2):
                for r in range(2):
                    w_ref[pl.ds(r * 4 + f * 2 + m, 256, stride=8), :] = new[f][
                        m * 256 : (m + 1) * 256, r * 128 : (r + 1) * 128
                    ]

    gate(0, 0)
    swap_outer(w_ref)
    gate(2, 1)
    swap_inner(w_ref)
    gate(4, 2)
    swap_outer(w_ref)
    gate(6, 3)
    swap_inner(w_ref)


def greet_all():
    qa, qb = lax.axis_index("qa"), lax.axis_index("qb")
    barrier = pltpu.get_barrier_semaphore()

    def greet(i, _):
        there = (lax.rem(qa + i // 32, 8), lax.rem(qb + lax.rem(i, 32), 32))
        pl.semaphore_signal(barrier, inc=1, device_id=there, device_id_type=MESH)
        return 0

    lax.fori_loop(1, N_DEV, greet, 0)
    pl.semaphore_wait(barrier, N_DEV - 1)


def tile(index):
    return pl.ds(pl.multiple_of(index * 8, 8), 8)


def send_all(src_ref, dst_ref, send_sem, recv_sem):
    qa, qb = lax.axis_index("qa"), lax.axis_index("qb")
    me = qa * N_QB + qb

    def send(i, _):
        a, b = lax.rem(qa + i // 32, 8), lax.rem(qb + lax.rem(i, 32), 32)
        pltpu.make_async_remote_copy(
            src_ref=src_ref.at[tile(a * N_QB + b)],
            dst_ref=dst_ref.at[tile(me)],
            send_sem=send_sem,
            recv_sem=recv_sem,
            device_id=(a, b),
            device_id_type=MESH,
        ).start()
        return 0

    lax.fori_loop(1, N_DEV, send, 0)
    dst_ref[tile(me), :] = src_ref[tile(me), :]


def await_rows(ref, rows, send_sem, recv_sem):
    qa, qb = lax.axis_index("qa"), lax.axis_index("qb")
    pltpu.make_async_remote_copy(
        src_ref=ref.at[pl.ds(0, rows)],
        dst_ref=ref.at[pl.ds(0, rows)],
        send_sem=send_sem,
        recv_sem=recv_sem,
        device_id=(qa, qb),
        device_id_type=MESH,
    ).wait()


def exchange_kernel(x_ref, o_ref, send_sem, recv_sem):
    greet_all()
    send_all(x_ref, o_ref, send_sem, recv_sem)
    await_rows(o_ref, ROWS - 8, send_sem, recv_sem)


def place():
    qa, qb = lax.axis_index("qa"), lax.axis_index("qb")
    return qb // 8, qa // 2, lax.rem(qa, 2) * 4 + lax.rem(qb // 2, 4), lax.rem(qb, 2)


def device(x, y, z, c):
    return (y * 2 + z // 4, x * 8 + lax.rem(z, 4) * 2 + c)


def rows_at(start, size):
    return pl.ds(pl.multiple_of(start, 8), size)


def reduce_all(part_ref, sum_ref, half_ref, quarter_ref, eighth_ref, columns_ref, acc_refs, send, recv):
    x, y, z, c = place()
    acc0, acc1, acc2 = acc_refs

    def put(stage, src, dst, there):
        pltpu.make_async_remote_copy(
            src_ref=src, dst_ref=dst, send_sem=send.at[stage], recv_sem=recv.at[stage],
            device_id=there, device_id_type=MESH,
        ).start()

    put(0, part_ref.at[rows_at((1 - c) * 640, 640)], half_ref, device(x, y, z, 1 - c))
    await_rows(half_ref, 640, send.at[0], recv.at[0])
    acc0[...] = part_ref[rows_at(c * 640, 640), :] + half_ref[...]
    for d in range(1, 4):
        to = lax.rem(x + d, 4)
        put(1, acc0.at[rows_at(to * 160, 160)], quarter_ref.at[pl.ds((d - 1) * 160, 160)], device(to, y, z, c))
    await_rows(quarter_ref, 480, send.at[1], recv.at[1])
    acc1[...] = (
        acc0[rows_at(x * 160, 160), :]
        + quarter_ref[0:160, :]
        + quarter_ref[160:320, :]
        + quarter_ref[320:480, :]
    )
    for d in range(1, 4):
        to = lax.rem(y + d, 4)
        put(2, acc1.at[rows_at(to * 40, 40)], eighth_ref.at[pl.ds((d - 1) * 40, 40)], device(x, to, z, c))
    await_rows(eighth_ref, 120, send.at[2], recv.at[2])
    acc2[...] = (
        acc1[rows_at(y * 40, 40), :] + eighth_ref[0:40, :] + eighth_ref[40:80, :] + eighth_ref[80:120, :]
    )
    for d in range(1, 8):
        put(3, acc2, columns_ref.at[rows_at(z * 40, 40)], device(x, y, lax.rem(z + d, 8), c))
    columns_ref[rows_at(z * 40, 40), :] = acc2[...]
    await_rows(columns_ref, 280, send.at[3], recv.at[3])
    total = columns_ref[0:40, :]
    for k in range(1, 8):
        total = total + columns_ref[k * 40 : (k + 1) * 40, :]
    mine = rows_at(c * 640 + x * 160 + y * 40, 40)
    sum_ref[mine, :] = total
    for d in range(1, 4):
        put(4, sum_ref.at[mine], sum_ref.at[mine], device(x, lax.rem(y + d, 4), z, c))
    await_rows(sum_ref, 120, send.at[4], recv.at[4])
    mine = rows_at(c * 640 + x * 160, 160)
    for d in range(1, 4):
        put(5, sum_ref.at[mine], sum_ref.at[mine], device(lax.rem(x + d, 4), y, z, c))
    await_rows(sum_ref, 480, send.at[5], recv.at[5])
    mine = rows_at(c * 640, 640)
    put(6, sum_ref.at[mine], sum_ref.at[mine], device(x, y, z, 1 - c))
    await_rows(sum_ref, 640, send.at[6], recv.at[6])


def last_exchange_kernel(
    x_ref, part_ref, o_ref, sum_ref, half_ref, quarter_ref, eighth_ref, columns_ref,
    acc0, acc1, acc2, send_sem, recv_sem, send, recv,
):
    greet_all()
    send_all(x_ref, o_ref, send_sem, recv_sem)
    reduce_all(
        part_ref, sum_ref, half_ref, quarter_ref, eighth_ref, columns_ref, (acc0, acc1, acc2), send, recv
    )
    await_rows(o_ref, ROWS - 8, send_sem, recv_sem)


def finish_kernel(scaling, r_ref, sum_ref, gates_ref, state_ref, adjoint_ref, grads_ref):
    for f, ref in enumerate((state_ref, adjoint_ref)):
        for r in range(2):
            for m in range(4):
                j = r * 4 + f * 2 + m // 2
                block = r_ref[pl.ds((m % 2) * 1024 + j, 128, stride=8), :]
                ref[r, pl.ds(m, 128, stride=4), :] = block.T
    for slot in range(4):
        for r in range(2):
            grads_ref[2 * slot, r] = scaling * sum_ref[pl.ds(slot * 256 + r * 128, 128), :]
    rho = scaling * jnp.concatenate(
        [sum_ref[pl.ds(1024, 128), :], sum_ref[pl.ds(1152, 128), :]], axis=1
    )
    for k in (1, 3, 5, 7):
        re, im = gates_ref[k, 0], gates_ref[k, 1]
        grad = dot3(rho, conj_embed(re, -im), 1, 0)
        grad_re, grad_im = grad[:, :128], grad[:, 128:]
        grads_ref[k, 0] = grad_re
        grads_ref[k, 1] = grad_im
        if k < 7:
            right = jnp.concatenate(
                [jnp.concatenate([grad_re, grad_im], axis=1), jnp.concatenate([grad_im, -grad_re], axis=1)],
                axis=0,
            )
            rho = dot3(jnp.concatenate([re, im], axis=0), right, 0, 0)


VMEM = pl.BlockSpec(memory_space=pltpu.VMEM)


def local_call(kernel, outs, *args):
    return pl.pallas_call(
        kernel,
        out_shape=[jax.ShapeDtypeStruct(s, F32) for s in outs],
        in_specs=[VMEM] * len(args),
        out_specs=[VMEM] * len(outs),
        compiler_params=pltpu.CompilerParams(vmem_limit_bytes=48 << 20),
    )(*args)


def shards(state, adjoint, gates):
    scaling = float(N_DEV * 65536 // 128) ** -0.5
    y, rho = local_call(
        low_kernel, [(ROWS, 128), (256, 128)], state.reshape(2, 512, 128), adjoint.reshape(2, 512, 128), gates
    )
    z = pl.pallas_call(
        exchange_kernel,
        out_shape=jax.ShapeDtypeStruct((ROWS, 128), F32),
        in_specs=[VMEM],
        out_specs=VMEM,
        scratch_shapes=[pltpu.SemaphoreType.DMA, pltpu.SemaphoreType.DMA],
        compiler_params=pltpu.CompilerParams(collective_id=0, has_side_effects=True),
    )(y)
    w, grads = local_call(high_kernel, [(ROWS, 128), (1024, 128)], z, gates)
    parts = jnp.concatenate([grads, rho], axis=0)
    r, sums = pl.pallas_call(
        last_exchange_kernel,
        out_shape=[jax.ShapeDtypeStruct((ROWS, 128), F32), jax.ShapeDtypeStruct((GROWS, 128), F32)],
        in_specs=[VMEM] * 2,
        out_specs=[VMEM] * 2,
        scratch_shapes=[
            pltpu.VMEM((640, 128), F32),
            pltpu.VMEM((480, 128), F32),
            pltpu.VMEM((120, 128), F32),
            pltpu.VMEM((320, 128), F32),
            pltpu.VMEM((640, 128), F32),
            pltpu.VMEM((160, 128), F32),
            pltpu.VMEM((40, 128), F32),
            pltpu.SemaphoreType.DMA,
            pltpu.SemaphoreType.DMA,
            pltpu.SemaphoreType.DMA((7,)),
            pltpu.SemaphoreType.DMA((7,)),
        ],
        compiler_params=pltpu.CompilerParams(collective_id=1, has_side_effects=True),
    )(w, parts)
    state_out, adjoint_out, grads_out = local_call(
        functools.partial(finish_kernel, scaling), [(2, 512, 128), (2, 512, 128), (8, 2, 128, 128)], r, sums, gates
    )
    return state_out.reshape(state.shape), adjoint_out.reshape(adjoint.shape), grads_out


def solution(mesh):
    in_specs = (P(None, "qa", "qb", None), P(None, "qa", "qb", None), P())
    out_specs = (P(None, "qa", "qb", None), P(None, "qa", "qb", None), P())
    return jax.shard_map(shards, mesh=mesh, in_specs=in_specs, out_specs=out_specs, check_vma=False)
```

time: 473 us -> 132 us (0.28); the launches traced: 466 us -> 132 us
  waiting for transfers between devices: 300 us -> 0 us
  Pallas kernels: 0 us -> 122 us
  matrix products: 55 us -> 0 us
  starting transfers between devices: 52 us -> 0 us
  local copies, waits for them, and re-layouts: 28.5 us -> 8.76 us
  between operations: 15.4 us -> 0.72 us
  other arithmetic: 15.5 us -> 0.91 us
    psum x1 -> x0, waiting for transfers between devices: 254 us -> none  [shards(): gradients = lax.psum(jnp.stack(collected), ('qa', 'qb'))]
    pallas_call x0 -> x5, Pallas kernels: none -> 122 us  [the longest x1 56.2 us: shards(): pl.pallas_call(last_exchange_kernel, out_shape=[jax.ShapeDtypeStruct((ROW...]
    dot_general x96 -> x0, matrix products: 55 us -> none  [contract(): lax.dot_general(left, right, (((left_dim,), (right_dim,)), ((), ())), pre...]
    all_to_all x6 -> x0, starting transfers between devices: 51.9 us -> none  [the longest x2 23.7 us: sent_together(): lax.all_to_all(both, axis, split_axis=split_dim, concat_axis=concat_dim,...]
    all_to_all x6 -> x0, waiting for transfers between devices: 45.8 us -> none  [the longest x2 17.3 us: sent_together(): lax.all_to_all(both, axis, split_axis=split_dim, concat_axis=concat_dim,...]
    slice x7 -> x0, local copies, waits for them, and re-layouts: 12.9 us -> none  [the longest x6 12.3 us: undo_high(): field[0]]
    another operation x5 -> x0, other arithmetic: 5.71 us -> none  [the longest x4 5.04 us: undo_low(): return jnp.stack([new_real, new_imag])]
    unnamed x7 -> x0, other arithmetic: 5.5 us -> none
  transfers between devices with their start and end apart: 7 -> 0, of which waited for: 6 -> 0; matrix products, arithmetic and copies ran while one was open for 10% -> 0% of each run, Pallas kernels for 0% -> 0%
where the time goes in v1:
time: 132 us
  Pallas kernels  122 us (92%)
  local copies, waits for them, and re-layouts  8.76 us (7%)
    pallas_call x1, Pallas kernels, shards(): pl.pallas_call(last_exchange_kernel, out_shape=[jax.ShapeDtypeStruct((ROW...  56.2 us
    pallas_call x1, Pallas kernels, shards(): pl.pallas_call(exchange_kernel, out_shape=jax.ShapeDtypeStruct((ROWS, 128...  43.4 us
    pallas_call x3, Pallas kernels, local_call(): pl.pallas_call(kernel, out_shape=[jax.ShapeDtypeStruct(s, F32) for s in o...  21.9 us
    unnamed x18, local copies, waits for them, and re-layouts  8.76 us

profile of v1, /device:TPU:1, one launch (start us, length us, event | category | flops | bytes accessed | tf_op | source)
XLA Modules:
  0.0 131.9 jit_solution(5376993584303509747)
XLA Ops:
  0.6 0.0 copy-start
  0.6 1.2 copy-done
  1.9 0.0 copy-start.7
  1.9 1.0 copy-done.7
  2.9 0.0 copy-start.8
  2.9 1.0 copy-done.8
  3.9 1.4 %shard_map.58 = (f32[2048,128]{1,0:T(8,128)S(1)}, f32[256,128]{1,0:T(8,128)S(1)}) custom-call(f32[2,512,128]{2,1,0:T(8,128)S(1)} %bitcast.4, f32[2,512,128]{2,1,0:T(8,128)S(1)} %bitcast.5, f32[8,2,128,128]{3,2,1,0:T(8,128)S(1)} %copy-done), custom_call_target="tpu_custom_call" | custom-call | tf_op jit(solution)/shard_map/pallas_call | solution.py:307
  5.3 0.0 copy-start.4
  5.3 1.0 copy-done.4
  6.3 0.0 copy-start.1
  6.3 43.4 %shard_map.59.z_ref = f32[2048,128]{1,0:T(8,128)} custom-call(f32[2048,128]{1,0:T(8,128)} %copy-done.4), custom_call_target="tpu_custom_call" | custom-call | tf_op jit(solution)/shard_map/pallas_call | solution.py:321
  49.7 0.0 copy-done.1
  49.7 0.0 copy-start.2
  49.7 1.2 copy-done.2
  50.9 17.9 %shard_map.60 = (f32[2048,128]{1,0:T(8,128)S(1)}, f32[1024,128]{1,0:T(8,128)S(1)}) custom-call(f32[2048,128]{1,0:T(8,128)S(1)} %copy-done.2, f32[8,2,128,128]{3,2,1,0:T(8,128)S(1)} %copy-done.1), custom_call_target="tpu_custom_call" | custom-call | tf_op jit(solution)/shard_map/pallas_call | solution.py:307
  68.8 0.0 copy-start.5
  68.8 1.0 copy-done.5
  69.8 0.9 pad_maximum_fusion.part_ref
  70.7 56.2 %shard_map.61 = (f32[2048,128]{1,0:T(8,128)}, f32[1280,128]{1,0:T(8,128)}) custom-call(f32[2048,128]{1,0:T(8,128)} %copy-done.5, f32[1280,128]{1,0:T(8,128)} %pad_maximum_fusion.part_ref), custom_call_target="tpu_custom_call" | custom-call | tf_op jit(solution)/shard_map/pallas_call | solution.py:331
  126.9 0.0 copy-start.3
  126.9 1.2 copy-done.3
  128.2 0.0 copy-start.6
  128.2 1.1 copy-done.6
  129.2 2.7 %shard_map.62 = (f32[2,512,128]{2,1,0:T(8,128)}, f32[2,512,128]{2,1,0:T(8,128)}, f32[8,2,128,128]{3,2,1,0:T(8,128)}) custom-call(f32[2048,128]{1,0:T(8,128)S(1)} %copy-done.3, f32[1280,128]{1,0:T(8,128)S(1)} %copy-done.6, f32[8,2,128,128]{3,2,1,0:T(8,128)S(1)} %copy-done.1), custom_call_target="tpu_custom_call" | custom-call | tf_op jit(solution)/shard_map/pallas_call | solution.py:307
Async XLA Ops:
  0.6 1.2 copy-start
  1.9 1.0 copy-start.7
  2.9 1.0 copy-start.8
  5.3 1.0 copy-start.4
  6.3 43.4 %copy-start.1 = (f32[8,2,128,128]{3,2,1,0:T(8,128)S(1)}, f32[8,2,128,128]{3,2,1,0:T(8,128)}, u32[]{:S(2)}) copy-start(f32[8,2,128,128]{3,2,1,0:T(8,128)} %gates_ref.5) | copy-start | bytes 3145732
  49.7 1.2 copy-start.2
  68.8 1.0 copy-start.5
  126.9 1.2 copy-start.3
  128.2 1.1 copy-start.6

commit v2 on v1

--- a/solution.py
+++ b/solution.py
@@ -34,112 +34,168 @@
     )
 
 
-def swap_bits(vs, shift):
-    vs = list(vs)
-    lane = lax.broadcasted_iota(jnp.int32, vs[0].shape, 1)
-    bit = 0
-    while (1 << bit) < len(vs):
-        stride = 1 << (shift + bit)
-        upper = (lane & stride) != 0
-        for i in range(len(vs)):
-            if i & (1 << bit):
-                continue
-            k = i | (1 << bit)
-            lo, hi = vs[i], vs[k]
-            vs[i] = jnp.where(upper, pltpu.roll(hi, stride, 1), lo)
-            vs[k] = jnp.where(upper, hi, pltpu.roll(lo, 128 - stride, 1))
-        bit += 1
-    return vs
-
-
-def swap_outer(ref):
-    def body(b, _):
-        at = [pl.ds(pl.multiple_of((a * 32 + b) * 8, 8), 8) for a in range(8)]
-        for s, v in zip(at, swap_bits([ref[s, :] for s in at], 4)):
-            ref[s, :] = v
-        return 0
-
-    lax.fori_loop(0, 32, body, 0, unroll=2)
-
-
-def swap_inner(ref):
-    def body(a, _):
-        at = [pl.ds(pl.multiple_of((a * 32 + b) * 8, 8), 8) for b in range(32)]
-        for s, v in zip(at, swap_bits([ref[s, :] for s in at], 2)):
-            ref[s, :] = v
-        return 0
-
-    lax.fori_loop(0, 8, body, 0)
+def undo_matrix(gates_ref, k):
+    re, im = gates_ref[k, 0].T, gates_ref[k, 1].T
+    hi, lo = split(
+        jnp.concatenate(
+            [jnp.concatenate([re, im], axis=1), jnp.concatenate([-im, re], axis=1)], axis=0
+        )
+    )
+    return jnp.concatenate([hi, lo, hi], axis=1)
+
+
+def undo(matrix, x):
+    hi, lo = split(x)
+    return jnp.dot(matrix, jnp.concatenate([hi, hi, lo], axis=0), preferred_element_type=F32)
 
 
 def quadrants(q):
     return q[:128, :128] + q[128:, 128:], q[128:, :128] - q[:128, 128:]
 
 
-def low_kernel(state_ref, adjoint_ref, gates_ref, y_ref, rho_ref):
-    fields = []
-    for ref in (state_ref, adjoint_ref):
-        fields.append(jnp.concatenate([ref[0], ref[1]], axis=1))
-    rho_re, rho_im = quadrants(dot3(fields[1], fields[0], 0, 0))
-    rho_ref[0:128, :] = rho_re
-    rho_ref[128:256, :] = rho_im
-    top = jnp.concatenate([gates_ref[1, 0], -gates_ref[1, 1]], axis=1)
+def cat(parts, axis):
+    return jnp.concatenate(list(parts), axis=axis)
+
+
+def store_gradient(part_ref, slot, q):
+    re, im = quadrants(q)
+    part_ref[pl.ds(slot * 256, 128), :] = re
+    part_ref[pl.ds(slot * 256 + 128, 128), :] = im
+
+
+def before_kernel(fields, gates_ref, x_ref, y_ref, part_ref):
+    matrix = undo_matrix(gates_ref, 0)
+    old = [
+        cat((cat((ref[r, pl.ds(m, 128, stride=4), :] for m in range(4)), 1) for r in range(2)), 0)
+        for ref in fields
+    ]
+    new = [undo(matrix, x) for x in old]
+    for f in range(2):
+        for r in range(2):
+            for m in range(4):
+                x_ref[pl.ds(((f * 2 + r) * 4 + m) * 128, 128), :] = new[f][
+                    r * 128 : (r + 1) * 128, m * 128 : (m + 1) * 128
+                ]
+    store_gradient(part_ref, 0, dot3(old[1], new[0], 1, 1))
+    flat = [cat((ref[0], ref[1]), 1) for ref in fields]
+    store_gradient(part_ref, 4, dot3(flat[1], flat[0], 0, 0))
+    top = cat((gates_ref[1, 0], -gates_ref[1, 1]), 1)
     for k in (3, 5, 7):
         top = dot3(top, conj_embed(gates_ref[k, 0], gates_ref[k, 1]), 1, 0)
-    joined = conj_embed(top[:, :128], -top[:, 128:])
-    for m in range(4):
-        rows = []
-        for ref in (state_ref, adjoint_ref):
-            rows.append(
-                jnp.concatenate([ref[r, pl.ds(m, 128, stride=4), :] for r in range(2)], axis=1)
-            )
-        out = dot3(joined, jnp.concatenate(rows, axis=0), 0, 1)
-        for r in range(2):
+    joined = cat((top[:, :128].T, top[:, 128:].T), 1)
+    for m0 in range(2):
+        straight, crossed = [], []
+        for t in range(8):
             for f in range(2):
-                j = r * 4 + f * 2 + m // 2
-                y_ref[pl.ds((m % 2) * 1024 + j, 128, stride=8), :] = out[
-                    r * 128 : (r + 1) * 128, f * 128 : (f + 1) * 128
+                for m1 in range(2):
+                    re, im = (
+                        x_ref[pl.ds(((f * 2 + r) * 4 + m1 * 2 + m0) * 128 + t * 16, 16), :]
+                        for r in range(2)
+                    )
+                    straight += [re, im]
+                    crossed += [-im, re]
+        out = dot3(joined, cat((cat(straight, 0), cat(crossed, 0)), 1), 1, 1)
+        for t in range(8):
+            y_ref[pl.ds(m0 * 1024 + (t % 2) * 4 + t // 2, 128, stride=8), :] = out[
+                :, t * 128 : (t + 1) * 128
+            ]
+
+
+def block1(t0, m1, f):
+    return ((t0 * 2 + m1) * 2 + f) * 256
+
+
+FOUR = [(t0, m1) for t0 in range(2) for m1 in range(2)]
+
+
+def load1(ref, f):
+    return cat((ref[pl.ds(block1(t0, m1, f), 256), :] for t0, m1 in FOUR), 1)
+
+
+def load2(ref, t):
+    return cat((ref[pl.ds(t * 256 + r, 128, stride=2), :] for r in range(2)), 0)
+
+
+def load3(ref, b1):
+    return cat(
+        (ref[pl.ds(t * 256 + b1 * 32 + r, 16, stride=2), :] for r in range(2) for t in range(8)), 0
+    )
+
+
+def between_kernel(z_ref, one_ref, one_new_ref, two_ref, two_new_ref, w_ref, matrices):
+    for a in range(8):
+        for t0 in range(2):
+            rows = cat((z_ref[pl.ds(a * 256 + t0 * 4 + t, 32, stride=8), :] for t in range(4)), 0).T
+            for f in range(2):
+                for m1 in range(2):
+                    for r in range(2):
+                        at = ((f * 2 + m1) * 2 + r) * 16
+                        one_ref[pl.ds(block1(t0, m1, f) + r * 128 + a * 16, 16), :] = rows[at : at + 16]
+    for f in range(2):
+        new = undo(matrices[0], load1(one_ref, f))
+        for i, (t0, m1) in enumerate(FOUR):
+            one_new_ref[pl.ds(block1(t0, m1, f), 256), :] = new[:, i * 128 : (i + 1) * 128]
+    for t0 in range(2):
+        for v in range(4):
+            for r in range(2):
+                rows = cat(
+                    (
+                        one_new_ref[pl.ds(block1(t0, m1, f) + r * 128 + v, 32, stride=4), :]
+                        for f in range(2)
+                        for m1 in range(2)
+                    ),
+                    0,
+                ).T
+                for t in range(4):
+                    two_ref[pl.ds((t * 2 + t0) * 256 + v * 2 + r, 32, stride=8), :] = rows[
+                        t * 32 : (t + 1) * 32
+                    ]
+    for half in range(2):
+        new = undo(matrices[1], cat((load2(two_ref, half * 4 + i) for i in range(4)), 1))
+        for i in range(4):
+            for r in range(2):
+                two_new_ref[pl.ds((half * 4 + i) * 256 + r, 128, stride=2), :] = new[
+                    r * 128 : (r + 1) * 128, i * 128 : (i + 1) * 128
                 ]
-
-
-def high_kernel(z_ref, gates_ref, w_ref, grad_ref):
-    w_ref[...] = z_ref[...]
-
-    def gate(index, slot):
-        embedded = conj_embed(gates_ref[index, 0], gates_ref[index, 1])
-        old = []
-        for f in range(2):
-            old.append(
-                jnp.concatenate(
-                    [
-                        jnp.concatenate(
-                            [w_ref[pl.ds(r * 4 + f * 2 + m, 256, stride=8), :] for r in range(2)],
-                            axis=1,
-                        )
-                        for m in range(2)
-                    ],
-                    axis=0,
-                )
-            )
-        new = [dot3(x, embedded, 1, 0) for x in old]
-        grad_re, grad_im = quadrants(dot3(old[1], new[0], 0, 0))
-        grad_ref[pl.ds(slot * 256, 128), :] = grad_re
-        grad_ref[pl.ds(slot * 256 + 128, 128), :] = grad_im
-        for f in range(2):
-            for m in range(2):
-                for r in range(2):
-                    w_ref[pl.ds(r * 4 + f * 2 + m, 256, stride=8), :] = new[f][
-                        m * 256 : (m + 1) * 256, r * 128 : (r + 1) * 128
-                    ]
-
-    gate(0, 0)
-    swap_outer(w_ref)
-    gate(2, 1)
-    swap_inner(w_ref)
-    gate(4, 2)
-    swap_outer(w_ref)
-    gate(6, 3)
-    swap_inner(w_ref)
+    for half in range(2):
+        new = undo(matrices[2], cat((load3(two_new_ref, half * 4 + i) for i in range(4)), 1))
+        for i in range(4):
+            for r in range(2):
+                w_ref[pl.ds((half * 4 + i) * 256 + r, 128, stride=2), :] = new[
+                    r * 128 : (r + 1) * 128, i * 128 : (i + 1) * 128
+                ]
+
+
+def lane_gradient(old, new):
+    upper = lax.broadcasted_iota(jnp.int32, (256, 128), 1) >= 64
+    total = None
+    for i in range(0, 8, 2):
+        left = jnp.where(upper, old[i](), pltpu.roll(old[i + 1](), 64, 1))
+        right = jnp.where(upper, pltpu.roll(new[i](), 64, 1), new[i + 1]())
+        q = dot3(left, right, 1, 1)
+        total = q if total is None else total + q
+    return total
+
+
+def gradients(part_ref, one_ref, one_new_ref, two_ref, two_new_ref, w_ref):
+    store_gradient(part_ref, 1, dot3(load1(one_ref, 1), load1(one_new_ref, 0), 1, 1))
+    each = range(8)
+    store_gradient(
+        part_ref,
+        2,
+        lane_gradient(
+            [functools.partial(load2, two_ref, t) for t in each],
+            [functools.partial(load2, two_new_ref, t) for t in each],
+        ),
+    )
+    store_gradient(
+        part_ref,
+        3,
+        lane_gradient(
+            [functools.partial(load3, two_new_ref, b) for b in each],
+            [functools.partial(load2, w_ref, b) for b in each],
+        ),
+    )
 
 
 def greet_all():
@@ -152,7 +208,10 @@
         return 0
 
     lax.fori_loop(1, N_DEV, greet, 0)
-    pl.semaphore_wait(barrier, N_DEV - 1)
+
+
+def await_all():
+    pl.semaphore_wait(pltpu.get_barrier_semaphore(), N_DEV - 1)
 
 
 def tile(index):
@@ -189,12 +248,6 @@
         device_id=(qa, qb),
         device_id_type=MESH,
     ).wait()
-
-
-def exchange_kernel(x_ref, o_ref, send_sem, recv_sem):
-    greet_all()
-    send_all(x_ref, o_ref, send_sem, recv_sem)
-    await_rows(o_ref, ROWS - 8, send_sem, recv_sem)
 
 
 def place():
@@ -261,25 +314,36 @@
     await_rows(sum_ref, 640, send.at[6], recv.at[6])
 
 
-def last_exchange_kernel(
-    x_ref, part_ref, o_ref, sum_ref, half_ref, quarter_ref, eighth_ref, columns_ref,
-    acc0, acc1, acc2, send_sem, recv_sem, send, recv,
+def main_kernel(
+    state_ref, adjoint_ref, gates_ref, r_ref, sum_ref,
+    x_ref, y_ref, z_ref, one_ref, one_new_ref, two_ref, two_new_ref, w_ref, part_ref,
+    half_ref, quarter_ref, eighth_ref, columns_ref, acc0, acc1, acc2,
+    sends, recvs, send, recv,
 ):
     greet_all()
-    send_all(x_ref, o_ref, send_sem, recv_sem)
+    before_kernel((state_ref, adjoint_ref), gates_ref, x_ref, y_ref, part_ref)
+    await_all()
+    send_all(y_ref, z_ref, sends.at[0], recvs.at[0])
+    matrices = [undo_matrix(gates_ref, k) for k in (2, 4, 6)]
+    await_rows(z_ref, ROWS - 8, sends.at[0], recvs.at[0])
+    between_kernel(z_ref, one_ref, one_new_ref, two_ref, two_new_ref, w_ref, matrices)
+    send_all(w_ref, r_ref, sends.at[1], recvs.at[1])
+    gradients(part_ref, one_ref, one_new_ref, two_ref, two_new_ref, w_ref)
     reduce_all(
         part_ref, sum_ref, half_ref, quarter_ref, eighth_ref, columns_ref, (acc0, acc1, acc2), send, recv
     )
-    await_rows(o_ref, ROWS - 8, send_sem, recv_sem)
+    await_rows(r_ref, ROWS - 8, sends.at[1], recvs.at[1])
 
 
 def finish_kernel(scaling, r_ref, sum_ref, gates_ref, state_ref, adjoint_ref, grads_ref):
-    for f, ref in enumerate((state_ref, adjoint_ref)):
-        for r in range(2):
-            for m in range(4):
-                j = r * 4 + f * 2 + m // 2
-                block = r_ref[pl.ds((m % 2) * 1024 + j, 128, stride=8), :]
-                ref[r, pl.ds(m, 128, stride=4), :] = block.T
+    for m0 in range(2):
+        for v in range(4):
+            for r in range(2):
+                rows = r_ref[pl.ds(m0 * 1024 + v * 2 + r, 128, stride=8), :].T
+                for f, ref in enumerate((state_ref, adjoint_ref)):
+                    for m1 in range(2):
+                        at = (f * 2 + m1) * 32
+                        ref[r, pl.ds(v * 4 + m1 * 2 + m0, 32, stride=16), :] = rows[at : at + 32]
     for slot in range(4):
         for r in range(2):
             grads_ref[2 * slot, r] = scaling * sum_ref[pl.ds(slot * 256 + r * 128, 128), :]
@@ -315,25 +379,15 @@
 
 def shards(state, adjoint, gates):
     scaling = float(N_DEV * 65536 // 128) ** -0.5
-    y, rho = local_call(
-        low_kernel, [(ROWS, 128), (256, 128)], state.reshape(2, 512, 128), adjoint.reshape(2, 512, 128), gates
-    )
-    z = pl.pallas_call(
-        exchange_kernel,
-        out_shape=jax.ShapeDtypeStruct((ROWS, 128), F32),
-        in_specs=[VMEM],
-        out_specs=VMEM,
-        scratch_shapes=[pltpu.SemaphoreType.DMA, pltpu.SemaphoreType.DMA],
-        compiler_params=pltpu.CompilerParams(collective_id=0, has_side_effects=True),
-    )(y)
-    w, grads = local_call(high_kernel, [(ROWS, 128), (1024, 128)], z, gates)
-    parts = jnp.concatenate([grads, rho], axis=0)
+    buffer = pltpu.VMEM((ROWS, 128), F32)
     r, sums = pl.pallas_call(
-        last_exchange_kernel,
+        main_kernel,
         out_shape=[jax.ShapeDtypeStruct((ROWS, 128), F32), jax.ShapeDtypeStruct((GROWS, 128), F32)],
-        in_specs=[VMEM] * 2,
+        in_specs=[VMEM] * 3,
         out_specs=[VMEM] * 2,
         scratch_shapes=[
+            *[buffer] * 8,
+            pltpu.VMEM((GROWS, 128), F32),
             pltpu.VMEM((640, 128), F32),
             pltpu.VMEM((480, 128), F32),
             pltpu.VMEM((120, 128), F32),
@@ -341,13 +395,15 @@
             pltpu.VMEM((640, 128), F32),
             pltpu.VMEM((160, 128), F32),
             pltpu.VMEM((40, 128), F32),
-            pltpu.SemaphoreType.DMA,
-            pltpu.SemaphoreType.DMA,
+            pltpu.SemaphoreType.DMA((2,)),
+            pltpu.SemaphoreType.DMA((2,)),
             pltpu.SemaphoreType.DMA((7,)),
             pltpu.SemaphoreType.DMA((7,)),
         ],
-        compiler_params=pltpu.CompilerParams(collective_id=1, has_side_effects=True),
-    )(w, parts)
+        compiler_params=pltpu.CompilerParams(
+            collective_id=0, has_side_effects=True, vmem_limit_bytes=40 << 20
+        ),
+    )(state.reshape(2, 512, 128), adjoint.reshape(2, 512, 128), gates)
     state_out, adjoint_out, grads_out = local_call(
         functools.partial(finish_kernel, scaling), [(2, 512, 128), (2, 512, 128), (8, 2, 128, 128)], r, sums, gates
     )

time: 132 us -> 95.8 us (0.73)
  Pallas kernels: 122 us -> 91.6 us
  local copies, waits for them, and re-layouts: 8.76 us -> 3.3 us
    pallas_call x3 -> x1, Pallas kernels: 21.9 us -> 3.03 us  [local_call(): pl.pallas_call(kernel, out_shape=[jax.ShapeDtypeStruct(s, F32) for s in o...]
    pallas_call x2 -> x1, Pallas kernels: 99.6 us -> 88.6 us  [shards(): pl.pallas_call(main_kernel, out_shape=[jax.ShapeDtypeStruct((ROWS, 128),...]
    unnamed x18 -> x8, local copies, waits for them, and re-layouts: 8.76 us -> 3.3 us
where the time goes in v2:
time: 95.8 us; the launch traced here: 95.6 us
  Pallas kernels  91.6 us (96%)
  local copies, waits for them, and re-layouts  3.3 us (3%)
    pallas_call x1, Pallas kernels, shards(): pl.pallas_call(main_kernel, out_shape=[jax.ShapeDtypeStruct((ROWS, 128),...  88.6 us
    unnamed x8, local copies, waits for them, and re-layouts  3.3 us
    pallas_call x1, Pallas kernels, local_call(): pl.pallas_call(kernel, out_shape=[jax.ShapeDtypeStruct(s, F32) for s in o...  3.03 us

profile of v2, /device:TPU:1, one launch (start us, length us, event | category | flops | bytes accessed | tf_op | source)
XLA Modules:
  0.0 95.6 jit_solution(15609910193068009770)
XLA Ops:
  0.6 0.0 copy-start
  0.6 1.2 %copy-done = f32[8,2,128,128]{3,2,1,0:T(8,128)S(1)} copy-done((f32[8,2,128,128]{3,2,1,0:T(8,128)S(1)}, f32[8,2,128,128]{3,2,1,0:T(8,128)}, u32[]{:S(2)}) %copy-start) | copy-done | bytes 1048600
  1.9 0.0 copy-start.2
  1.9 1.0 %copy-done.2 = f32[2,1,1,65536]{3,2,1,0:T(1,128)S(1)} copy-done((f32[2,1,1,65536]{3,2,1,0:T(1,128)S(1)}, f32[2,1,1,65536]{3,2,1,0:T(1,128)}, u32[]{:S(2)}) %copy-start.2) | copy-done | bytes 524312
  2.9 0.0 copy-start.3
  2.9 1.0 %copy-done.3 = f32[2,1,1,65536]{3,2,1,0:T(1,128)S(1)} copy-done((f32[2,1,1,65536]{3,2,1,0:T(1,128)S(1)}, f32[2,1,1,65536]{3,2,1,0:T(1,128)}, u32[]{:S(2)}) %copy-start.3) | copy-done | bytes 524312
  3.9 0.0 copy-start.1
  3.9 88.6 %shard_map.58 = (f32[2048,128]{1,0:T(8,128)S(1)}, f32[1280,128]{1,0:T(8,128)S(1)}) custom-call(f32[2,512,128]{2,1,0:T(8,128)S(1)} %bitcast.4, f32[2,512,128]{2,1,0:T(8,128)S(1)} %bitcast.5, f32[8,2,128,128]{3,2,1,0:T(8,128)S(1)} %copy-done), custom_call_target="tpu_custom_call" | custom-call | tf_op jit(solution)/shard_map/pallas_call | solution.py:383
  92.6 0.0 copy-done.1
  92.6 3.0 %shard_map.59 = (f32[2,512,128]{2,1,0:T(8,128)}, f32[2,512,128]{2,1,0:T(8,128)}, f32[8,2,128,128]{3,2,1,0:T(8,128)}) custom-call(f32[2048,128]{1,0:T(8,128)S(1)} %get-tuple-element.8.r_ref, f32[1280,128]{1,0:T(8,128)S(1)} %get-tuple-element.9.sum_ref, f32[8,2,128,128]{3,2,1,0:T(8,128)S(1)} %copy-done.1), custom_call_target="tpu_custom_call" | custom-call | tf_op jit(solution)/shard_map/pallas_call | solution.py:371
Async XLA Ops:
  0.6 1.2 %copy-start = (f32[8,2,128,128]{3,2,1,0:T(8,128)S(1)}, f32[8,2,128,128]{3,2,1,0:T(8,128)}, u32[]{:S(2)}) copy-start(f32[8,2,128,128]{3,2,1,0:T(8,128)} %gates_ref.3) | copy-start | bytes 3145732
  1.9 1.0 %copy-start.2 = (f32[2,1,1,65536]{3,2,1,0:T(1,128)S(1)}, f32[2,1,1,65536]{3,2,1,0:T(1,128)}, u32[]{:S(2)}) copy-start(f32[2,1,1,65536]{3,2,1,0:T(1,128)} %param.3) | copy-start | bytes 1572868
  2.9 1.0 %copy-start.3 = (f32[2,1,1,65536]{3,2,1,0:T(1,128)S(1)}, f32[2,1,1,65536]{3,2,1,0:T(1,128)}, u32[]{:S(2)}) copy-start(f32[2,1,1,65536]{3,2,1,0:T(1,128)} %param.4) | copy-start | bytes 1572868
  3.9 88.6 %copy-start.1 = (f32[8,2,128,128]{3,2,1,0:T(8,128)S(1)}, f32[8,2,128,128]{3,2,1,0:T(8,128)}, u32[]{:S(2)}) copy-start(f32[8,2,128,128]{3,2,1,0:T(8,128)} %gates_ref.3) | copy-start | bytes 3145732

commit v3 on v2

v3 whole, which is shorter than its diff:
```python
import functools

import jax
import jax.numpy as jnp
from jax import lax
from jax.experimental import pallas as pl
from jax.experimental.pallas import tpu as pltpu
from jax.sharding import PartitionSpec as P

F32 = jnp.float32
BF16 = jnp.bfloat16
MESH = pl.DeviceIdType.MESH
N_QA, N_QB, N_DEV = 8, 32, 256
HALF = N_DEV * 4
GROWS = 5 * 256


def split(x):
    hi = x.astype(BF16)
    return hi, (x - hi.astype(F32)).astype(BF16)


def dot3(a, b, ca, cb):
    ah, al = split(a)
    bh, bl = split(b)
    left = jnp.concatenate([ah, al, ah], axis=ca)
    right = jnp.concatenate([bh, bh, bl], axis=cb)
    return lax.dot_general(left, right, (((ca,), (cb,)), ((), ())), preferred_element_type=F32)


def conj_embed(re, im):
    return jnp.concatenate(
        [jnp.concatenate([re, -im], axis=1), jnp.concatenate([im, re], axis=1)], axis=0
    )


def undo_matrix(gates_ref, k):
    re, im = gates_ref[k, 0].T, gates_ref[k, 1].T
    hi, lo = split(
        jnp.concatenate(
            [jnp.concatenate([re, im], axis=1), jnp.concatenate([-im, re], axis=1)], axis=0
        )
    )
    return jnp.concatenate([hi, lo, hi], axis=1)


def undo_lanes_matrix(gates_ref, k):
    hi, lo = split(jnp.concatenate([gates_ref[k, 0].T, gates_ref[k, 1].T], axis=1))
    return jnp.concatenate([hi, lo, hi], axis=1)


def undo(matrix, x):
    hi, lo = split(x)
    return jnp.dot(matrix, jnp.concatenate([hi, hi, lo], axis=0), preferred_element_type=F32)


def quadrants(q):
    return q[:128, :128] + q[128:, 128:], q[128:, :128] - q[:128, 128:]


def cat(parts, axis):
    return jnp.concatenate(list(parts), axis=axis)


def store_gradient(part_ref, slot, re, im):
    part_ref[pl.ds(slot * 256, 128), :] = re
    part_ref[pl.ds(slot * 256 + 128, 128), :] = im


def before_kernel(fields, gates_ref, x_ref, y_refs, part_ref):
    matrix = undo_matrix(gates_ref, 0)
    old = [
        cat((cat((ref[r, pl.ds(m, 128, stride=4), :] for m in range(4)), 1) for r in range(2)), 0)
        for ref in fields
    ]
    new = [undo(matrix, x) for x in old]
    for f in range(2):
        for r in range(2):
            for m in range(4):
                x_ref[pl.ds(((f * 2 + r) * 4 + m) * 128, 128), :] = new[f][
                    r * 128 : (r + 1) * 128, m * 128 : (m + 1) * 128
                ]
    store_gradient(part_ref, 0, *quadrants(dot3(old[1], new[0], 1, 1)))
    flat = [cat((ref[0], ref[1]), 1) for ref in fields]
    store_gradient(part_ref, 1, *quadrants(dot3(flat[1], flat[0], 0, 0)))
    top = cat((gates_ref[1, 0], -gates_ref[1, 1]), 1)
    for k in (3, 5, 7):
        top = dot3(top, conj_embed(gates_ref[k, 0], gates_ref[k, 1]), 1, 0)
    joined = cat((top[:, :128].T, top[:, 128:].T), 1)
    for m1 in range(2):
        for m0 in range(2):
            straight, crossed = [], []
            for t21 in range(4):
                for f in range(2):
                    for t0 in range(2):
                        re, im = (
                            x_ref[
                                pl.ds(((f * 2 + r) * 4 + m1 * 2 + m0) * 128 + (t21 * 2 + t0) * 16, 16), :
                            ]
                            for r in range(2)
                        )
                        straight += [re, im]
                        crossed += [-im, re]
            out = dot3(joined, cat((cat(straight, 0), cat(crossed, 0)), 1), 1, 1)
            for t21 in range(4):
                y_refs[m1][pl.ds(m0 * 512 + t21, 128, stride=4), :] = out[:, t21 * 128 : (t21 + 1) * 128]


def turned(x):
    upper = lax.broadcasted_iota(jnp.int32, x.shape, 1) >= 64
    rolled = pltpu.roll(x, 64, 1)
    return jnp.where(upper, -rolled, rolled)


def load1(ref, f):
    return cat((ref[pl.ds((t0 * 2 + f) * 256, 256), :] for t0 in range(2)), 1)


def load2(ref, t):
    return ref[pl.ds(t * 128, 128), :]


def load3(ref, b1):
    return cat((ref[pl.ds(t * 128 + b1 * 16, 16), :] for t in range(8)), 0)


def undo_lanes(matrix, load):
    blocks = [load(i) for i in range(8)]
    return undo(matrix, cat((cat(blocks, 1), cat((turned(x) for x in blocks), 1)), 0))


def between_kernel(z_ref, one_ref, one_new_ref, two_ref, two_new_ref, w_ref, matrices, after=lambda k: None):
    for a in range(8):
        rows = cat((z_ref[pl.ds(a * 128 + t, 32, stride=4), :] for t in range(4)), 0).T
        for f in range(2):
            for t0 in range(2):
                for r in range(2):
                    at = ((f * 2 + t0) * 2 + r) * 16
                    one_ref[pl.ds((t0 * 2 + f) * 256 + r * 128 + a * 16, 16), :] = rows[at : at + 16]
    new = undo(matrices[0], cat((load1(one_ref, f) for f in range(2)), 1))
    for f in range(2):
        for t0 in range(2):
            one_new_ref[pl.ds((t0 * 2 + f) * 256, 256), :] = new[
                :, (f * 2 + t0) * 128 : (f * 2 + t0 + 1) * 128
            ]
    after(0)
    for t0 in range(2):
        for v in range(4):
            rows = cat(
                (
                    one_new_ref[pl.ds((t0 * 2 + f) * 256 + r * 128 + v, 32, stride=4), :]
                    for r in range(2)
                    for f in range(2)
                ),
                0,
            ).T
            for t in range(4):
                two_ref[pl.ds((t * 2 + t0) * 128 + v, 32, stride=4), :] = rows[t * 32 : (t + 1) * 32]
    new = undo_lanes(matrices[1], functools.partial(load2, two_ref))
    for t in range(8):
        two_new_ref[pl.ds(t * 128, 128), :] = new[:, t * 128 : (t + 1) * 128]
    after(1)
    new = undo_lanes(matrices[2], functools.partial(load3, two_new_ref))
    for b1 in range(8):
        w_ref[pl.ds(b1 * 128, 128), :] = new[:, b1 * 128 : (b1 + 1) * 128]
    after(2)


def lane_gradient(load_old, old_ref, load_new, new_ref):
    lane = lax.broadcasted_iota(jnp.int32, (128, 128), 1)
    adjoint = (lane & 32) != 0
    lefts, rights, crosses = [], [], []
    for i in range(0, 8, 2):
        lefts.append(
            jnp.where(adjoint, load_old(old_ref, i), pltpu.roll(load_old(old_ref, i + 1), 96, 1))
        )
        right = jnp.where(adjoint, pltpu.roll(load_new(new_ref, i), 32, 1), load_new(new_ref, i + 1))
        rights.append(right)
        crosses.append(-turned(right))
    q = dot3(cat(lefts, 1), cat((cat(rights, 1), cat(crosses, 1)), 0), 1, 1)
    return q[:, :128], q[:, 128:]


def gradient(k, one_ref, one_new_ref, two_ref, two_new_ref, w_ref):
    if k == 0:
        return quadrants(dot3(load1(one_ref, 1), load1(one_new_ref, 0), 1, 1))
    if k == 1:
        return lane_gradient(load2, two_ref, load2, two_new_ref)
    return lane_gradient(load3, two_new_ref, load2, w_ref)


def low_gradients(scaling, sum_ref, gates_ref, low_ref):
    rho = scaling * cat((sum_ref[pl.ds(256, 128), :], sum_ref[pl.ds(384, 128), :]), 1)
    for i, k in enumerate((1, 3, 5, 7)):
        re, im = gates_ref[k, 0], gates_ref[k, 1]
        grad = dot3(rho, conj_embed(re, -im), 1, 0)
        grad_re, grad_im = grad[:, :128], grad[:, 128:]
        low_ref[i, 0] = grad_re
        low_ref[i, 1] = grad_im
        if k < 7:
            right = cat((cat((grad_re, grad_im), 1), cat((grad_im, -grad_re), 1)), 0)
            rho = dot3(cat((re, im), 0), right, 0, 0)


def greet_all():
    qa, qb = lax.axis_index("qa"), lax.axis_index("qb")
    barrier = pltpu.get_barrier_semaphore()

    def greet(i, _):
        there = (lax.rem(qa + i // 32, 8), lax.rem(qb + lax.rem(i, 32), 32))
        pl.semaphore_signal(barrier, inc=1, device_id=there, device_id_type=MESH)
        return 0

    lax.fori_loop(1, N_DEV, greet, 0)


def await_all():
    pl.semaphore_wait(pltpu.get_barrier_semaphore(), N_DEV - 1)


def tile(index):
    return pl.ds(pl.multiple_of(index * 4, 4), 4)


def send_blocks(src_ref, dst_ref, send_sem, recv_sem, first=0, last=N_DEV):
    qa, qb = lax.axis_index("qa"), lax.axis_index("qb")
    me = qa * N_QB + qb

    def send(i, _):
        a, b = lax.rem(qa + i // 32, 8), lax.rem(qb + lax.rem(i, 32), 32)
        pltpu.make_async_remote_copy(
            src_ref=src_ref.at[tile(a * N_QB + b)],
            dst_ref=dst_ref.at[tile(me)],
            send_sem=send_sem,
            recv_sem=recv_sem,
            device_id=(a, b),
            device_id_type=MESH,
        ).start()
        return 0

    lax.fori_loop(max(first, 1), last, send, 0)
    if first == 0:
        dst_ref[tile(me), :] = src_ref[tile(me), :]


def await_rows(ref, rows, send_sem, recv_sem):
    qa, qb = lax.axis_index("qa"), lax.axis_index("qb")
    pltpu.make_async_remote_copy(
        src_ref=ref.at[pl.ds(0, rows)],
        dst_ref=ref.at[pl.ds(0, rows)],
        send_sem=send_sem,
        recv_sem=recv_sem,
        device_id=(qa, qb),
        device_id_type=MESH,
    ).wait()


def place():
    qa, qb = lax.axis_index("qa"), lax.axis_index("qb")
    return qb // 8, qa // 2, lax.rem(qa, 2) * 4 + lax.rem(qb // 2, 4), lax.rem(qb, 2)


def device(x, y, z, c):
    return (y * 2 + z // 4, x * 8 + lax.rem(z, 4) * 2 + c)


def rows_at(start, size):
    return pl.ds(pl.multiple_of(start, 8), size)


class GradientSum:
    def __init__(self, part_ref, sum_ref, slots, refs, send, recv):
        self.part, self.sum, self.slots = part_ref, sum_ref, slots
        self.got, self.mine, self.columns = refs
        self.send, self.recv = send, recv
        self.x, self.y, self.z, self.c = place()
        self.piece = self.y * 8 + self.x * 2 + self.c

    def put(self, stage, src, dst, there):
        pltpu.make_async_remote_copy(
            src_ref=src, dst_ref=dst, send_sem=self.send.at[stage], recv_sem=self.recv.at[stage],
            device_id=device(*there), device_id_type=MESH,
        ).start()

    def plane(self, body):
        def step(d, _):
            other = lax.rem(self.piece + d, 32)
            body(d, other, (lax.rem(other // 2, 4), other // 8, self.z, lax.rem(other, 2)))
            return 0

        lax.fori_loop(1, 32, step, 0)

    def rows(self, slot, piece):
        return rows_at(slot * 256 + piece * 8, 8)

    def start_slot(self, i):
        def body(d, other, there):
            self.put(i, self.part.at[self.rows(self.slots[i], other)], self.got.at[rows_at((i * 32 + d) * 8, 8)], there)

        self.plane(body)

    def start_columns(self):
        n = len(self.slots)
        for i, slot in enumerate(self.slots):
            await_rows(self.got, 31 * 8, self.send.at[i], self.recv.at[i])
            total = self.part[self.rows(slot, self.piece), :]
            for d in range(1, 32):
                total = total + self.got[(i * 32 + d) * 8 : (i * 32 + d + 1) * 8, :]
            self.mine[i * 8 : (i + 1) * 8, :] = total
        here = rows_at(self.z * n * 8, n * 8)
        for d in range(1, 8):
            self.put(n, self.mine, self.columns.at[here], (self.x, self.y, lax.rem(self.z + d, 8), self.c))
        self.columns[here, :] = self.mine[...]

    def start_plane(self):
        n = len(self.slots)
        await_rows(self.columns, 7 * n * 8, self.send.at[n], self.recv.at[n])
        for i, slot in enumerate(self.slots):
            total = self.columns[i * 8 : (i + 1) * 8, :]
            for k in range(1, 8):
                total = total + self.columns[(k * n + i) * 8 : (k * n + i + 1) * 8, :]
            self.sum[self.rows(slot, self.piece), :] = total

        def body(d, other, there):
            for slot in self.slots:
                mine = self.sum.at[self.rows(slot, self.piece)]
                self.put(n + 1, mine, mine, there)

        self.plane(body)

    def finish(self):
        n = len(self.slots)
        await_rows(self.sum, 31 * n * 8, self.send.at[n + 1], self.recv.at[n + 1])


def sum_scratch(slots):
    return [pltpu.VMEM((n * slots, 128), F32) for n in (256, 8, 64)]


def main_kernel(
    scaling,     state_hbm, adjoint_hbm, gates_hbm, r0_ref, r1_ref, sum_ref, low_ref,
    state_ref, adjoint_ref, gates_ref, x_ref,
    y0, y1, z0, z1, w0, w1, one0, one1, one_new0, one_new1, two0, two1, two_new0, two_new1, part_ref,
    a1, a2, a3, b1, b2, b3,
    loads, sends, recvs, send_a, recv_a, send_b, recv_b,
):
    pairs = ((state_hbm, state_ref), (adjoint_hbm, adjoint_ref), (gates_hbm, gates_ref))
    copies = [pltpu.make_async_copy(src, dst, loads.at[i]) for i, (src, dst) in enumerate(pairs)]
    for copy in copies:
        copy.start()
    greet_all()
    for copy in copies:
        copy.wait()
    before_kernel((state_ref, adjoint_ref), gates_ref, x_ref, (y0, y1), part_ref)
    early = GradientSum(part_ref, sum_ref, (0, 1), (a1, a2, a3), send_a, recv_a)
    late = GradientSum(part_ref, sum_ref, (2, 3, 4), (b1, b2, b3), send_b, recv_b)
    one = (one0, one_new0, two0, two_new0, w0)
    two = (one1, one_new1, two1, two_new1, w1)
    await_all()
    early.start_slot(0)
    early.start_slot(1)
    send_blocks(y0, z0, sends.at[0], recvs.at[0])
    send_blocks(y1, z1, sends.at[1], recvs.at[1])
    matrices = [undo_matrix(gates_ref, 2)] + [undo_lanes_matrix(gates_ref, k) for k in (4, 6)]
    early.start_columns()
    await_rows(z0, HALF - 4, sends.at[0], recvs.at[0])
    between_kernel(z0, *one, matrices)
    send_blocks(w0, r0_ref, sends.at[2], recvs.at[2])
    first = [gradient(k, *one) for k in range(3)]
    early.start_plane()
    await_rows(z1, HALF - 4, sends.at[1], recvs.at[1])

    def after(k):
        (re0, im0), (re1, im1) = first[k], gradient(k, *two)
        store_gradient(part_ref, 2 + k, re0 + re1, im0 + im1)
        late.start_slot(k)

    between_kernel(z1, *two, matrices, after)
    send_blocks(w1, r1_ref, sends.at[3], recvs.at[3], 0, 128)
    late.start_columns()
    send_blocks(w1, r1_ref, sends.at[3], recvs.at[3], 128, N_DEV)
    early.finish()
    low_gradients(scaling, sum_ref, gates_ref, low_ref)
    late.start_plane()
    late.finish()
    for i, r_ref in enumerate((r0_ref, r1_ref)):
        await_rows(r_ref, HALF - 4, sends.at[2 + i], recvs.at[2 + i])


def finish_kernel(scaling, r0_ref, r1_ref, sum_ref, low_ref, state_ref, adjoint_ref, grads_ref):
    for m1, from_ref in enumerate((r0_ref, r1_ref)):
        for m0 in range(2):
            for v in range(4):
                rows = from_ref[pl.ds(m0 * 512 + v, 128, stride=4), :].T
                for r in range(2):
                    for f, ref in enumerate((state_ref, adjoint_ref)):
                        at = (r * 2 + f) * 32
                        ref[r, pl.ds(v * 4 + m1 * 2 + m0, 32, stride=16), :] = rows[at : at + 32]
    for k, slot in ((0, 0), (2, 2), (4, 3), (6, 4)):
        for r in range(2):
            grads_ref[k, r] = scaling * sum_ref[pl.ds(slot * 256 + r * 128, 128), :]
    for i in range(4):
        grads_ref[2 * i + 1] = low_ref[i]


VMEM = pl.BlockSpec(memory_space=pltpu.VMEM)


def local_call(kernel, outs, *args):
    return pl.pallas_call(
        kernel,
        out_shape=[jax.ShapeDtypeStruct(s, F32) for s in outs],
        in_specs=[VMEM] * len(args),
        out_specs=[VMEM] * len(outs),
        compiler_params=pltpu.CompilerParams(vmem_limit_bytes=48 << 20),
    )(*args)


def shards(state, adjoint, gates):
    scaling = float(N_DEV * 65536 // 128) ** -0.5
    half = pltpu.VMEM((HALF, 128), F32)
    hbm = pl.BlockSpec(memory_space=pltpu.HBM)
    received = jax.ShapeDtypeStruct((HALF, 128), F32)
    r0, r1, sums, low = pl.pallas_call(
        functools.partial(main_kernel, scaling),
        out_shape=[
            received,
            received,
            jax.ShapeDtypeStruct((GROWS, 128), F32),
            jax.ShapeDtypeStruct((4, 2, 128, 128), F32),
        ],
        in_specs=[hbm] * 3,
        out_specs=[VMEM] * 4,
        scratch_shapes=[
            pltpu.VMEM((2, 512, 128), F32),
            pltpu.VMEM((2, 512, 128), F32),
            pltpu.VMEM((8, 2, 128, 128), F32),
            pltpu.VMEM((2048, 128), F32),
            *[half] * 14,
            pltpu.VMEM((GROWS, 128), F32),
            *sum_scratch(2),
            *sum_scratch(3),
            pltpu.SemaphoreType.DMA((3,)),
            pltpu.SemaphoreType.DMA((4,)),
            pltpu.SemaphoreType.DMA((4,)),
            *[pltpu.SemaphoreType.DMA((5,))] * 4,
        ],
        compiler_params=pltpu.CompilerParams(
            collective_id=0, has_side_effects=True, vmem_limit_bytes=40 << 20
        ),
    )(state.reshape(2, 512, 128), adjoint.reshape(2, 512, 128), gates)
    state_out, adjoint_out, grads_out = local_call(
        functools.partial(finish_kernel, scaling),
        [(2, 512, 128), (2, 512, 128), (8, 2, 128, 128)],
        r0, r1, sums, low,
    )
    return state_out.reshape(state.shape), adjoint_out.reshape(adjoint.shape), grads_out


def solution(mesh):
    in_specs = (P(None, "qa", "qb", None), P(None, "qa", "qb", None), P())
    out_specs = (P(None, "qa", "qb", None), P(None, "qa", "qb", None), P())
    return jax.shard_map(shards, mesh=mesh, in_specs=in_specs, out_specs=out_specs, check_vma=False)
```

time: 95.8 us -> 81.1 us (0.85)
  Pallas kernels: 91.6 us -> 76.9 us
    pallas_call x1, Pallas kernels: 88.6 us -> 75.1 us  [shards(): pl.pallas_call(functools.partial(main_kernel, scaling), out_shape=[receiv...]
    pallas_call x1, Pallas kernels: 3.03 us -> 1.8 us  [local_call(): pl.pallas_call(kernel, out_shape=[jax.ShapeDtypeStruct(s, F32) for s in o...]
    unnamed x8 -> x6, local copies, waits for them, and re-layouts: 3.3 us -> 3.3 us
where the time goes in v3:
time: 81.1 us; the launch traced here: 80.9 us
  Pallas kernels  76.9 us (95%)
  local copies, waits for them, and re-layouts  3.3 us (4%)
    pallas_call x1, Pallas kernels, shards(): pl.pallas_call(functools.partial(main_kernel, scaling), out_shape=[receiv...  75.1 us
    unnamed x6, local copies, waits for them, and re-layouts  3.3 us
    pallas_call x1, Pallas kernels, local_call(): pl.pallas_call(kernel, out_shape=[jax.ShapeDtypeStruct(s, F32) for s in o...  1.8 us

profile of v3, /device:TPU:1, one launch (start us, length us, event | category | flops | bytes accessed | tf_op | source)
XLA Modules:
  0.0 80.9 jit_solution(15440766781975939409)
XLA Ops:
  0.6 0.0 copy-start
  0.6 1.2 %copy-done = f32[8,2,128,128]{3,2,1,0:T(8,128)S(1)} copy-done((f32[8,2,128,128]{3,2,1,0:T(8,128)S(1)}, f32[8,2,128,128]{3,2,1,0:T(8,128)}, u32[]{:S(2)}) %copy-start) | copy-done | bytes 1048600
  1.9 0.0 copy-start.1
  1.9 1.0 %copy-done.1 = f32[2,1,1,65536]{3,2,1,0:T(1,128)S(1)} copy-done((f32[2,1,1,65536]{3,2,1,0:T(1,128)S(1)}, f32[2,1,1,65536]{3,2,1,0:T(1,128)}, u32[]{:S(2)}) %copy-start.1) | copy-done | bytes 524312
  2.9 0.0 copy-start.2
  2.9 1.0 %copy-done.2 = f32[2,1,1,65536]{3,2,1,0:T(1,128)S(1)} copy-done((f32[2,1,1,65536]{3,2,1,0:T(1,128)S(1)}, f32[2,1,1,65536]{3,2,1,0:T(1,128)}, u32[]{:S(2)}) %copy-start.2) | copy-done | bytes 524312
  3.9 75.1 %shard_map.58 = (f32[1024,128]{1,0:T(8,128)S(1)}, f32[1024,128]{1,0:T(8,128)S(1)}, f32[1280,128]{1,0:T(8,128)S(1)}, f32[4,2,128,128]{3,2,1,0:T(8,128)S(1)}) custom-call(f32[2,512,128]{2,1,0:T(8,128)S(1)} %bitcast.4, f32[2,512,128]{2,1,0:T(8,128)S(1)} %bitcast.5, f32[8,2,128,128]{3,2,1,0:T(8,128)S(1)} %copy-done), custom_call_target="tpu_custom_call" | custom-call | tf_op jit(solution)/shard_map/pallas_call | solution.py:424
  79.1 1.8 %shard_map.59 = (f32[2,512,128]{2,1,0:T(8,128)}, f32[2,512,128]{2,1,0:T(8,128)}, f32[8,2,128,128]{3,2,1,0:T(8,128)}) custom-call(f32[1024,128]{1,0:T(8,128)S(1)} %get-tuple-element.10.r0_ref, f32[1024,128]{1,0:T(8,128)S(1)} %get-tuple-element.11.r1_ref, f32[1280,128]{1,0:T(8,128)S(1)} %get-tuple-element.12.sum_ref, ...), custom_call_target="tpu_custom_call" | custom-call | tf_op jit(solution)/shard_map/pallas_call | solution.py:410
Async XLA Ops:
  0.6 1.2 %copy-start = (f32[8,2,128,128]{3,2,1,0:T(8,128)S(1)}, f32[8,2,128,128]{3,2,1,0:T(8,128)}, u32[]{:S(2)}) copy-start(f32[8,2,128,128]{3,2,1,0:T(8,128)} %gates_hbm.1) | copy-start | bytes 3145732
  1.9 1.0 %copy-start.1 = (f32[2,1,1,65536]{3,2,1,0:T(1,128)S(1)}, f32[2,1,1,65536]{3,2,1,0:T(1,128)}, u32[]{:S(2)}) copy-start(f32[2,1,1,65536]{3,2,1,0:T(1,128)} %param.3) | copy-start | bytes 1572868
  2.9 1.0 %copy-start.2 = (f32[2,1,1,65536]{3,2,1,0:T(1,128)S(1)}, f32[2,1,1,65536]{3,2,1,0:T(1,128)}, u32[]{:S(2)}) copy-start(f32[2,1,1,65536]{3,2,1,0:T(1,128)} %param.4) | copy-start | bytes 1572868

commit v4 on v3

--- a/solution.py
+++ b/solution.py
@@ -67,43 +67,52 @@
     part_ref[pl.ds(slot * 256 + 128, 128), :] = im
 
 
-def before_kernel(fields, gates_ref, x_ref, y_refs, part_ref):
+def undo_first(fields, gates_ref, x_ref):
     matrix = undo_matrix(gates_ref, 0)
-    old = [
-        cat((cat((ref[r, pl.ds(m, 128, stride=4), :] for m in range(4)), 1) for r in range(2)), 0)
-        for ref in fields
-    ]
-    new = [undo(matrix, x) for x in old]
-    for f in range(2):
+    for f, ref in enumerate(fields):
+        old = cat(
+            (cat((ref[r, pl.ds(m, 128, stride=4), :] for m in range(4)), 1) for r in range(2)), 0
+        )
+        new = undo(matrix, old)
         for r in range(2):
             for m in range(4):
-                x_ref[pl.ds(((f * 2 + r) * 4 + m) * 128, 128), :] = new[f][
+                x_ref[pl.ds(((f * 2 + r) * 4 + m) * 128, 128), :] = new[
                     r * 128 : (r + 1) * 128, m * 128 : (m + 1) * 128
                 ]
-    store_gradient(part_ref, 0, *quadrants(dot3(old[1], new[0], 1, 1)))
-    flat = [cat((ref[0], ref[1]), 1) for ref in fields]
-    store_gradient(part_ref, 1, *quadrants(dot3(flat[1], flat[0], 0, 0)))
+
+
+def join_low(gates_ref):
     top = cat((gates_ref[1, 0], -gates_ref[1, 1]), 1)
     for k in (3, 5, 7):
         top = dot3(top, conj_embed(gates_ref[k, 0], gates_ref[k, 1]), 1, 0)
-    joined = cat((top[:, :128].T, top[:, 128:].T), 1)
-    for m1 in range(2):
-        for m0 in range(2):
-            straight, crossed = [], []
-            for t21 in range(4):
-                for f in range(2):
-                    for t0 in range(2):
-                        re, im = (
-                            x_ref[
-                                pl.ds(((f * 2 + r) * 4 + m1 * 2 + m0) * 128 + (t21 * 2 + t0) * 16, 16), :
-                            ]
-                            for r in range(2)
-                        )
-                        straight += [re, im]
-                        crossed += [-im, re]
-            out = dot3(joined, cat((cat(straight, 0), cat(crossed, 0)), 1), 1, 1)
-            for t21 in range(4):
-                y_refs[m1][pl.ds(m0 * 512 + t21, 128, stride=4), :] = out[:, t21 * 128 : (t21 + 1) * 128]
+    return cat((top[:, :128].T, top[:, 128:].T), 1)
+
+
+def undo_low(joined, m1, x_ref, y_ref):
+    for m0 in range(2):
+        straight, crossed = [], []
+        for t21 in range(4):
+            for f in range(2):
+                for t0 in range(2):
+                    re, im = (
+                        x_ref[pl.ds(((f * 2 + r) * 4 + m1 * 2 + m0) * 128 + (t21 * 2 + t0) * 16, 16), :]
+                        for r in range(2)
+                    )
+                    straight += [re, im]
+                    crossed += [-im, re]
+        out = dot3(joined, cat((cat(straight, 0), cat(crossed, 0)), 1), 1, 1)
+        for t21 in range(4):
+            y_ref[pl.ds(m0 * 512 + t21, 128, stride=4), :] = out[:, t21 * 128 : (t21 + 1) * 128]
+
+
+def first_gradients(fields, x_ref, part_ref):
+    old = cat(
+        (cat((fields[1][r, pl.ds(m, 128, stride=4), :] for m in range(4)), 1) for r in range(2)), 0
+    )
+    new = cat((cat((x_ref[pl.ds((r * 4 + m) * 128, 128), :] for m in range(4)), 1) for r in range(2)), 0)
+    store_gradient(part_ref, 0, *quadrants(dot3(old, new, 1, 1)))
+    flat = [cat((ref[0], ref[1]), 1) for ref in fields]
+    store_gradient(part_ref, 1, *quadrants(dot3(flat[1], flat[0], 0, 0)))
 
 
 def turned(x):
@@ -207,11 +216,12 @@
     barrier = pltpu.get_barrier_semaphore()
 
     def greet(i, _):
-        there = (lax.rem(qa + i // 32, 8), lax.rem(qb + lax.rem(i, 32), 32))
+        there = (lax.rem(qa + i // 32 + 4, 8), lax.rem(qb + lax.rem(i, 32) + 16, 32))
         pl.semaphore_signal(barrier, inc=1, device_id=there, device_id_type=MESH)
         return 0
 
-    lax.fori_loop(1, N_DEV, greet, 0)
+    lax.fori_loop(0, 144, greet, 0)
+    lax.fori_loop(145, N_DEV, greet, 0)
 
 
 def await_all():
@@ -346,20 +356,26 @@
 ):
     pairs = ((state_hbm, state_ref), (adjoint_hbm, adjoint_ref), (gates_hbm, gates_ref))
     copies = [pltpu.make_async_copy(src, dst, loads.at[i]) for i, (src, dst) in enumerate(pairs)]
-    for copy in copies:
+    for copy in reversed(copies):
         copy.start()
     greet_all()
-    for copy in copies:
-        copy.wait()
-    before_kernel((state_ref, adjoint_ref), gates_ref, x_ref, (y0, y1), part_ref)
+    fields = (state_ref, adjoint_ref)
+    copies[2].wait()
+    joined = join_low(gates_ref)
+    copies[0].wait()
+    copies[1].wait()
+    undo_first(fields, gates_ref, x_ref)
+    undo_low(joined, 0, x_ref, y0)
     early = GradientSum(part_ref, sum_ref, (0, 1), (a1, a2, a3), send_a, recv_a)
     late = GradientSum(part_ref, sum_ref, (2, 3, 4), (b1, b2, b3), send_b, recv_b)
     one = (one0, one_new0, two0, two_new0, w0)
     two = (one1, one_new1, two1, two_new1, w1)
     await_all()
+    send_blocks(y0, z0, sends.at[0], recvs.at[0])
+    first_gradients(fields, x_ref, part_ref)
     early.start_slot(0)
     early.start_slot(1)
-    send_blocks(y0, z0, sends.at[0], recvs.at[0])
+    undo_low(joined, 1, x_ref, y1)
     send_blocks(y1, z1, sends.at[1], recvs.at[1])
     matrices = [undo_matrix(gates_ref, 2)] + [undo_lanes_matrix(gates_ref, k) for k in (4, 6)]
     early.start_columns()
@@ -378,7 +394,7 @@
     between_kernel(z1, *two, matrices, after)
     send_blocks(w1, r1_ref, sends.at[3], recvs.at[3], 0, 128)
     late.start_columns()
-    send_blocks(w1, r1_ref, sends.at[3], recvs.at[3], 128, N_DEV)
+    send_blocks(w1, r1_ref, sends.at[3], recvs.at[3], 128, 256)
     early.finish()
     low_gradients(scaling, sum_ref, gates_ref, low_ref)
     late.start_plane()
@@ -420,6 +436,7 @@
     scaling = float(N_DEV * 65536 // 128) ** -0.5
     half = pltpu.VMEM((HALF, 128), F32)
     hbm = pl.BlockSpec(memory_space=pltpu.HBM)
+    inputs = (state.reshape(2, 512, 128), adjoint.reshape(2, 512, 128), gates)
     received = jax.ShapeDtypeStruct((HALF, 128), F32)
     r0, r1, sums, low = pl.pallas_call(
         functools.partial(main_kernel, scaling),
@@ -448,7 +465,7 @@
         compiler_params=pltpu.CompilerParams(
             collective_id=0, has_side_effects=True, vmem_limit_bytes=40 << 20
         ),
-    )(state.reshape(2, 512, 128), adjoint.reshape(2, 512, 128), gates)
+    )(*(pltpu.with_memory_space_constraint(v, pltpu.HBM) for v in inputs))
     state_out, adjoint_out, grads_out = local_call(
         functools.partial(finish_kernel, scaling),
         [(2, 512, 128), (2, 512, 128), (8, 2, 128, 128)],

time: 81.1 us -> 78.1 us (0.963)
  local copies, waits for them, and re-layouts: 3.3 us -> 0 us
    unnamed x6 -> x0, local copies, waits for them, and re-layouts: 3.3 us -> none
where the time goes in v4:
time: 78.1 us; the launch traced here: 78 us
  Pallas kernels  77.4 us (99%)
    pallas_call x1, Pallas kernels, shards(): pl.pallas_call(functools.partial(main_kernel, scaling), out_shape=[receiv...  75.6 us
    pallas_call x1, Pallas kernels, local_call(): pl.pallas_call(kernel, out_shape=[jax.ShapeDtypeStruct(s, F32) for s in o...  1.8 us

profile of v4, /device:TPU:1, one launch (start us, length us, event | category | flops | bytes accessed | tf_op | source)
XLA Modules:
  0.0 78.0 jit_solution(13935439132076482814)
XLA Ops:
  0.6 75.6 %shard_map.58 = (f32[1024,128]{1,0:T(8,128)S(1)}, f32[1024,128]{1,0:T(8,128)S(1)}, f32[1280,128]{1,0:T(8,128)S(1)}, f32[4,2,128,128]{3,2,1,0:T(8,128)S(1)}) custom-call(f32[2,512,128]{2,1,0:T(8,128)} %bitcast.4, f32[2,512,128]{2,1,0:T(8,128)} %bitcast.5, f32[8,2,128,128]{3,2,1,0:T(8,128)} %gates_hbm.1), custom_call_target="tpu_custom_call" | custom-call | tf_op jit(solution)/shard_map/pallas_call | solution.py:441
  76.2 1.8 %shard_map.59 = (f32[2,512,128]{2,1,0:T(8,128)}, f32[2,512,128]{2,1,0:T(8,128)}, f32[8,2,128,128]{3,2,1,0:T(8,128)}) custom-call(f32[1024,128]{1,0:T(8,128)S(1)} %get-tuple-element.10.r0_ref, f32[1024,128]{1,0:T(8,128)S(1)} %get-tuple-element.11.r1_ref, f32[1280,128]{1,0:T(8,128)S(1)} %get-tuple-element.12.sum_ref, ...), custom_call_target="tpu_custom_call" | custom-call | tf_op jit(solution)/shard_map/pallas_call | solution.py:426

commit v5 on v4

--- a/solution.py
+++ b/solution.py
@@ -378,12 +378,11 @@
     undo_low(joined, 1, x_ref, y1)
     send_blocks(y1, z1, sends.at[1], recvs.at[1])
     matrices = [undo_matrix(gates_ref, 2)] + [undo_lanes_matrix(gates_ref, k) for k in (4, 6)]
-    early.start_columns()
     await_rows(z0, HALF - 4, sends.at[0], recvs.at[0])
     between_kernel(z0, *one, matrices)
     send_blocks(w0, r0_ref, sends.at[2], recvs.at[2])
+    early.start_columns()
     first = [gradient(k, *one) for k in range(3)]
-    early.start_plane()
     await_rows(z1, HALF - 4, sends.at[1], recvs.at[1])
 
     def after(k):
@@ -393,11 +392,12 @@
 
     between_kernel(z1, *two, matrices, after)
     send_blocks(w1, r1_ref, sends.at[3], recvs.at[3], 0, 128)
+    early.start_plane()
     late.start_columns()
     send_blocks(w1, r1_ref, sends.at[3], recvs.at[3], 128, 256)
+    late.start_plane()
     early.finish()
     low_gradients(scaling, sum_ref, gates_ref, low_ref)
-    late.start_plane()
     late.finish()
     for i, r_ref in enumerate((r0_ref, r1_ref)):
         await_rows(r_ref, HALF - 4, sends.at[2 + i], recvs.at[2 + i])

time: 78.1 us -> 74.5 us (0.954)
  Pallas kernels: 77.4 us -> 73.8 us
    pallas_call x1, Pallas kernels: 75.6 us -> 72 us  [shards(): pl.pallas_call(functools.partial(main_kernel, scaling), out_shape=[receiv...]
where the time goes in v5:
time: 74.5 us; the launch traced here: 74.4 us
  Pallas kernels  73.8 us (99%)
    pallas_call x1, Pallas kernels, shards(): pl.pallas_call(functools.partial(main_kernel, scaling), out_shape=[receiv...  72 us
    pallas_call x1, Pallas kernels, local_call(): pl.pallas_call(kernel, out_shape=[jax.ShapeDtypeStruct(s, F32) for s in o...  1.8 us

profile of v5, /device:TPU:1, one launch (start us, length us, event | category | flops | bytes accessed | tf_op | source)
XLA Modules:
  0.0 74.4 jit_solution(14289458435511267395)
XLA Ops:
  0.6 72.0 %shard_map.58 = (f32[1024,128]{1,0:T(8,128)S(1)}, f32[1024,128]{1,0:T(8,128)S(1)}, f32[1280,128]{1,0:T(8,128)S(1)}, f32[4,2,128,128]{3,2,1,0:T(8,128)S(1)}) custom-call(f32[2,512,128]{2,1,0:T(8,128)} %bitcast.4, f32[2,512,128]{2,1,0:T(8,128)} %bitcast.5, f32[8,2,128,128]{3,2,1,0:T(8,128)} %gates_hbm.1), custom_call_target="tpu_custom_call" | custom-call | tf_op jit(solution)/shard_map/pallas_call | solution.py:441
  72.6 1.8 %shard_map.59 = (f32[2,512,128]{2,1,0:T(8,128)}, f32[2,512,128]{2,1,0:T(8,128)}, f32[8,2,128,128]{3,2,1,0:T(8,128)}) custom-call(f32[1024,128]{1,0:T(8,128)S(1)} %get-tuple-element.10.r0_ref, f32[1024,128]{1,0:T(8,128)S(1)} %get-tuple-element.11.r1_ref, f32[1280,128]{1,0:T(8,128)S(1)} %get-tuple-element.12.sum_ref, ...), custom_call_target="tpu_custom_call" | custom-call | tf_op jit(solution)/shard_map/pallas_call | solution.py:426

commit v6 on v5

--- a/solution.py
+++ b/solution.py
@@ -392,9 +392,9 @@
 
     between_kernel(z1, *two, matrices, after)
     send_blocks(w1, r1_ref, sends.at[3], recvs.at[3], 0, 128)
-    early.start_plane()
     late.start_columns()
     send_blocks(w1, r1_ref, sends.at[3], recvs.at[3], 128, 256)
+    early.start_plane()
     late.start_plane()
     early.finish()
     low_gradients(scaling, sum_ref, gates_ref, low_ref)

time: 74.5 us -> 75.1 us (level)
  no operation moved by 1% of the time
where the time goes in v6:
time: 75.1 us; the launch traced here: 74.6 us
  Pallas kernels  74 us (99%)
    pallas_call x1, Pallas kernels, shards(): pl.pallas_call(functools.partial(main_kernel, scaling), out_shape=[receiv...  72.2 us
    pallas_call x1, Pallas kernels, local_call(): pl.pallas_call(kernel, out_shape=[jax.ShapeDtypeStruct(s, F32) for s in o...  1.8 us

profile of v6, /device:TPU:1, one launch (start us, length us, event | category | flops | bytes accessed | tf_op | source)
XLA Modules:
  0.0 74.6 jit_solution(7105750559600262808)
XLA Ops:
  0.6 72.2 %shard_map.58 = (f32[1024,128]{1,0:T(8,128)S(1)}, f32[1024,128]{1,0:T(8,128)S(1)}, f32[1280,128]{1,0:T(8,128)S(1)}, f32[4,2,128,128]{3,2,1,0:T(8,128)S(1)}) custom-call(f32[2,512,128]{2,1,0:T(8,128)} %bitcast.4, f32[2,512,128]{2,1,0:T(8,128)} %bitcast.5, f32[8,2,128,128]{3,2,1,0:T(8,128)} %gates_hbm.1), custom_call_target="tpu_custom_call" | custom-call | tf_op jit(solution)/shard_map/pallas_call | solution.py:441
  72.8 1.8 %shard_map.59 = (f32[2,512,128]{2,1,0:T(8,128)}, f32[2,512,128]{2,1,0:T(8,128)}, f32[8,2,128,128]{3,2,1,0:T(8,128)}) custom-call(f32[1024,128]{1,0:T(8,128)S(1)} %get-tuple-element.10.r0_ref, f32[1024,128]{1,0:T(8,128)S(1)} %get-tuple-element.11.r1_ref, f32[1280,128]{1,0:T(8,128)S(1)} %get-tuple-element.12.sum_ref, ...), custom_call_target="tpu_custom_call" | custom-call | tf_op jit(solution)/shard_map/pallas_call | solution.py:426
